TPU v7x, 32 devices: a whole 2x2x4 slice. The times are simulated.
32 devices in a mesh: seq: 4 (over x, core), fsdp: 8 (over z, y).
Axes of the slice: x: 2, y: 2, z: 4, core: 2. Of those that a mesh axis runs over, the one named last changes fastest.
Arguments:
- hidden_in: bfloat16 [8, 1024, 1536], P('fsdp', 'seq'), may hold values from -6 to 6
- positions: int32 [8, 1024], P('fsdp', 'seq'), may hold values from 0 to 5116, as said below
- attn_gain: bfloat16 [1536], P('fsdp'), may hold values from 0.25 to 1.75
- qkv_weight: bfloat16 [1536, 2048], P('fsdp'), may hold values from -0.15625 to 0.15625
- qkv_bias: bfloat16 [2048], P('fsdp'), may hold values from -3 to 3
- out_weight: bfloat16 [1536, 1536], P('fsdp'), may hold values from -1.75 to 1.75
- mlp_gain: bfloat16 [1536], P('fsdp'), may hold values from 0.25 to 1.75
- gate_weight: bfloat16 [8960, 1536], P('fsdp'), may hold values from -0.15625 to 0.15625
- up_weight: bfloat16 [8960, 1536], P('fsdp'), may hold values from -0.15625 to 0.15625
- down_weight: bfloat16 [8960, 1536], P('fsdp'), may hold values from -0.0625 to 0.0625
- cotangent: bfloat16 [8, 1024, 1536], P('fsdp', 'seq'), may hold values from -6 to 6
Outputs:
- hidden_out: bfloat16 [8, 1024, 1536], P('fsdp', 'seq')
- grad_in: float32 [8, 1024, 1536], P('fsdp', 'seq')
- grad_attn_gain: float32 [1536], P('fsdp')
- grad_qkv_weight: float32 [1536, 2048], P('fsdp')
- grad_qkv_bias: float32 [2048], P('fsdp')
- grad_out_weight: float32 [1536, 1536], P('fsdp')
- grad_mlp_gain: float32 [1536], P('fsdp')
- grad_gate_weight: float32 [8960, 1536], P('fsdp')
- grad_up_weight: float32 [8960, 1536], P('fsdp')
- grad_down_weight: float32 [8960, 1536], P('fsdp')
Inputs may be any that keep to these rules, and one draw needn't show every extreme that they name: Along each sequence the positions rise by 1 to 3 from one token to the next; the first lies below 2048.
All inputs are finite; a program needn't handle non-finite values.
Results may differ from a plain program's by a relative error of at most 0.019.
Values may be sent and summed in bfloat16 or wider, within the bound.
A program may use at most 320 MiB of HBM per device.

v0:
```python
import functools
import math

import jax
import jax.numpy as jnp
from jax import lax
from jax.experimental import pallas as pl
from jax.experimental.pallas import tpu as pltpu
from jax.sharding import PartitionSpec as P

HEADS = 12
KV_HEADS = 2
HEAD_DIM = 128


norm_eps = 1e-06
rope_base = 1000000.0


def rope_tables(position_row):
    half_dim = HEAD_DIM // 2
    frequency = jnp.exp(
        -(jnp.arange(half_dim, dtype=jnp.float32) * 2.0 / HEAD_DIM) * math.log(rope_base)
    )
    angles = position_row.astype(jnp.float32)[:, None] * frequency[None, :]
    angles = jnp.concatenate([angles, angles], axis=-1)
    return (jnp.cos(angles), jnp.sin(angles))


def rotate(values, cosine, sine):
    half_dim = values.shape[-1] // 2
    turned = jnp.concatenate([-values[..., half_dim:], values[..., :half_dim]], axis=-1)
    return values * cosine[:, None, :] + turned * sine[:, None, :]


def unrotate(grads_rot, cosine, sine):
    half_dim = grads_rot.shape[-1] // 2
    scaled = grads_rot * sine[:, None, :]
    return grads_rot * cosine[:, None, :] + jnp.concatenate(
        [scaled[..., half_dim:], -scaled[..., :half_dim]], axis=-1
    )


def norm_forward(values, gain):
    inverse = lax.rsqrt(jnp.mean(values * values, axis=-1, keepdims=True) + norm_eps)
    unit_rows = values * inverse
    return (unit_rows, inverse, (unit_rows * gain).astype(jnp.bfloat16))


def norm_backward(grad_normed, unit_rows, inverse, gain):
    grad_unit = grad_normed * gain
    grad_values = inverse * (
        grad_unit - unit_rows * jnp.mean(grad_unit * unit_rows, axis=-1, keepdims=True)
    )
    grad_gain = jnp.sum(grad_normed * unit_rows, axis=0)
    return (grad_values, grad_gain)


def masked_scores(queries, keys, block_start, block_rows):
    length = keys.shape[0]
    query_block = lax.dynamic_slice_in_dim(queries, block_start, block_rows, 0)
    scores = jnp.einsum(
        "bhd,ld->hbl", query_block, keys, preferred_element_type=jnp.float32
    ) * HEAD_DIM ** (-0.5)
    row_index = block_start + jnp.arange(block_rows)
    column_index = jnp.arange(length)
    allowed = column_index[None, :] <= row_index[:, None]
    return (query_block, jnp.where(allowed[None], scores, -1e30))


def attend_forward(queries, keys, values):
    length = keys.shape[0]
    block_rows = min(512, length)
    block_count = length // block_rows

    def one_block(block_start):
        query_block, scores = masked_scores(queries, keys, block_start, block_rows)
        row_max = jnp.max(scores, axis=-1, keepdims=True)
        exponent = jnp.exp(scores - row_max)
        row_total = jnp.sum(exponent, axis=-1, keepdims=True)
        probability = (exponent / row_total).astype(jnp.bfloat16)
        result = jnp.einsum("hbl,ld->bhd", probability, values, preferred_element_type=jnp.float32)
        return (result.astype(jnp.bfloat16), (row_max + jnp.log(row_total))[..., 0])

    results, log_totals = lax.map(one_block, jnp.arange(block_count) * block_rows)
    return (results.reshape(length, queries.shape[1], queries.shape[2]), log_totals)


def attend_backward(queries, keys, values, log_totals, grad_out):
    length = keys.shape[0]
    block_rows = min(512, length)
    block_count = length // block_rows
    score_scale = HEAD_DIM ** (-0.5)

    def one_block(running, inputs):
        grad_keys, grad_values = running
        block_start, log_block = inputs
        query_block, scores = masked_scores(queries, keys, block_start, block_rows)
        grad_block = lax.dynamic_slice_in_dim(grad_out, block_start, block_rows, 0)
        probability = jnp.exp(scores - log_block[..., None])
        grad_probs = jnp.einsum(
            "bhd,ld->hbl", grad_block, values, preferred_element_type=jnp.float32
        )
        row_delta = jnp.sum(probability * grad_probs, axis=-1, keepdims=True)
        grad_scores = (probability * (grad_probs - row_delta)).astype(jnp.bfloat16)
        grad_query = (
            jnp.einsum("hbl,ld->bhd", grad_scores, keys, preferred_element_type=jnp.float32)
            * score_scale
        )
        grad_keys = (
            grad_keys
            + jnp.einsum(
                "hbl,bhd->ld", grad_scores, query_block, preferred_element_type=jnp.float32
            )
            * score_scale
        )
        grad_values = grad_values + jnp.einsum(
            "hbl,bhd->ld",
            probability.astype(jnp.bfloat16),
            grad_block,
            preferred_element_type=jnp.float32,
        )
        return ((grad_keys, grad_values), grad_query)

    zero_rows = jnp.zeros((length, keys.shape[1]), jnp.float32)
    (grad_keys, grad_values), grad_query = lax.scan(
        one_block, (zero_rows, zero_rows), (jnp.arange(block_count) * block_rows, log_totals)
    )
    return (grad_query.reshape(queries.shape), grad_keys, grad_values)


MESH = pl.DeviceIdType.MESH
VMEM_BYTES = 67_000_000
NN = (((1,), (0,)), ((), ()))
NT = (((1,), (1,)), ((), ()))
TN = (((0,), (0,)), ((), ()))


def matmul(left, right, dims):
    return lax.dot_general(left, right, dims, preferred_element_type=jnp.float32)


def ring_place(index, size):
    side = index % 2
    return (index // 2) * (1 - side) + (size - 1 - index // 2) * side


def ring_member(place, size):
    side = place // (size // 2)
    return 2 * (place * (1 - side) + (size - 1 - place) * side) + side


def seq_partners(seq):
    core = seq + 1 - 2 * (seq % 2)
    far = (seq + 2) % 4
    return core, far, (core + 2) % 4


def greet(targets):
    barrier = pltpu.get_barrier_semaphore()
    for target in targets:
        pl.semaphore_signal(barrier, inc=1, device_id=target, device_id_type=MESH)
    pl.semaphore_wait(barrier, len(targets))


def for_blocks(width, block, body):
    for at in range(0, width, block):
        body(pl.ds(at, min(block, width - at)))


def loop_blocks(width, block, body):
    @pl.loop(0, width // block)
    def _(at):
        body(pl.ds(pl.multiple_of(at * block, block), block))


def turn_tables(trig):
    lane = lax.broadcasted_iota(jnp.int32, trig.shape, 1)
    swapped = pltpu.roll(trig, HEAD_DIM // 2, 1)
    first = lane < HEAD_DIM // 2
    return jnp.where(first, trig, swapped), jnp.where(first, -swapped, trig)


def head_columns(at):
    return slice(at * HEAD_DIM, (at + 1) * HEAD_DIM)


def causal(scores, start):
    rows = lax.broadcasted_iota(jnp.int32, scores.shape, 0) + start
    columns = lax.broadcasted_iota(jnp.int32, scores.shape, 1)
    return jnp.where(columns <= rows, scores, -1e30)


def inverse_of(values):
    return lax.rsqrt(jnp.mean(values * values, axis=-1, keepdims=True) + norm_eps)


def attend_forward_kernel(
    size,
    block,
    bias_share,
    rows_ref,
    trig_ref,
    piece_ref,
    small_ref,
    cot_ref,
    normed_out,
    heads_out,
    attended_out,
    log_out,
    piece_out,
    proj_out,
    trig_out,
    gains_out,
    normed_two_out,
    resid_out,
    cots_out,
    rows_all,
    trig_all,
    pieces,
    proj,
    smalls,
    cots,
    normed,
    heads,
    attended,
    logs,
    part,
    gains,
    bias,
    resid,
    seq_in,
    far_sum,
    normed_two,
    load_sems,
    store_sems,
    ring_sems,
    small_sems,
    cot_sems,
    cot_store_sems,
    seq_sems,
    sum_sems,
    proj_send,
    proj_recv,
):
    f32, bf16 = jnp.float32, jnp.bfloat16
    depth, joint = piece_ref.shape
    tokens, width = rows_ref.shape
    half = depth // 2
    cot_half = tokens // 2
    own = proj.shape[0]
    used = joint - own
    count = own // HEAD_DIM
    length = part.shape[0]
    per_group = own // depth
    scale = HEAD_DIM**-0.5
    me = lax.axis_index("fsdp")
    seq = lax.axis_index("seq")
    place = ring_place(me, size)
    right = ring_member((place + 1) % size, size)
    left = ring_member((place + size - 1) % size, size)
    core, far, diagonal = seq_partners(seq)
    ring = ({"fsdp": right}, {"fsdp": left})

    def remote(source, target, sems, at, device):
        return pltpu.make_async_remote_copy(
            src_ref=source,
            dst_ref=target,
            send_sem=sems.at[(0,) + at],
            recv_sem=sems.at[(1,) + at],
            device_id=device,
            device_id_type=MESH,
        )

    loads = [
        pltpu.make_async_copy(piece_ref, pieces.at[pl.ds(pl.multiple_of(me * depth, 16), depth)], load_sems.at[0]),
        pltpu.make_async_copy(trig_ref, trig_all.at[seq], load_sems.at[1]),
        pltpu.make_async_copy(rows_ref, rows_all.at[seq], load_sems.at[2]),
        pltpu.make_async_copy(small_ref, smalls.at[me], load_sems.at[3]),
        pltpu.make_async_copy(cot_ref, cots.at[me], load_sems.at[4]),
    ]
    for load in loads:
        load.start()
    greet(ring + ({"seq": core}, {"seq": far}, {"seq": diagonal}))

    def piece_of(step, side):
        return ring_member((place + size - step if side == 0 else place + step) % size, size)

    def ring_copy(step, side, sub):
        part_rows = half // 2
        start = piece_of(step, side) * depth + side * half + sub * part_rows
        span = pieces.at[pl.ds(pl.multiple_of(start, 16), part_rows)]
        return remote(span, span, ring_sems, (side, sub, step), ring[side])

    def small_copy(step):
        span = smalls.at[piece_of(step, 0)]
        return remote(span, span, small_sems, (step,), ring[0])

    def cot_copy(step, side, sub):
        part_rows = cot_half // 2
        start = side * cot_half + sub * part_rows
        span = cots.at[piece_of(step, side), pl.ds(start, part_rows)]
        return remote(span, span, cot_sems, (side, sub, step), ring[side])

    def cot_store(step, side):
        span = (piece_of(step, side), pl.ds(side * cot_half, cot_half))
        return pltpu.make_async_copy(
            cots.at[span], cots_out.at[span], cot_store_sems.at[side, step]
        )

    def seq_copy(which, block_at, target, at):
        span = (rows_all, trig_all)[which].at[block_at]
        return remote(span, span, seq_sems, (which, at), {"seq": target})

    def proj_part(step, side):
        at = piece_of(step, side)
        row = pl.multiple_of((at % per_group) * depth + side * half, 16)
        source = pieces.at[
            pl.ds(pl.multiple_of(at * depth + side * half, 16), half), pl.ds(used, own)
        ]
        target = proj.at[pl.ds(row, half), pl.ds(pl.multiple_of(seq * own, 128), own)]
        return at, at // per_group, source, target

    def proj_copy(step, side):
        at, owner, source, target = proj_part(step, side)
        return owner, pltpu.make_async_remote_copy(
            src_ref=source,
            dst_ref=target,
            send_sem=proj_send.at[side, step],
            recv_sem=proj_recv.at[seq, at % per_group, side],
            device_id={"seq": owner},
            device_id_type=MESH,
        )

    def proj_act(step, side, action):
        owner, copy = proj_copy(step, side)

        @pl.when(owner != seq)
        def _():
            if action == "start":
                copy.start()
            else:
                copy.wait_send()

        @pl.when(owner == seq)
        def _():
            _, _, source, target = proj_part(step, side)
            kept = pltpu.make_async_copy(source, target, proj_send.at[side, step])
            if action == "start":
                kept.start()
            else:
                kept.wait()

    stores = []

    def store(source, target):
        stores.append(pltpu.make_async_copy(source, target, store_sems.at[len(stores)]))
        stores[-1].start()

    def cot_pump(step):
        for sub in range(2):
            for side in range(2):
                if step >= 1:
                    cot_copy(step - 1, side, sub).wait_recv()
                if step < size - 1:
                    cot_copy(step, side, sub).start()
        for side in range(2):
            cot_store(step, side).start()

    loads[0].wait()
    for sub in range(2):
        for side in range(2):
            ring_copy(0, side, sub).start()
    loads[3].wait()
    small_copy(0).start()
    for which in (1, 0):
        loads[2 - which].wait()
        seq_copy(which, seq, far, 1).start()
        seq_copy(which, seq, core, 0).start()
    for side in range(2):
        proj_act(0, side, "start")
    loads[4].wait()

    for step in range(size - 1):
        for sub in range(2):
            for side in range(2):
                ring_copy(step, side, sub).wait_recv()
                if step < size - 2:
                    ring_copy(step + 1, side, sub).start()
        small_copy(step).wait_recv()
        if step < size - 2:
            small_copy(step + 1).start()
        if step == size - 3:
            cot_pump(0)
        for side in range(2):
            proj_act(step + 1, side, "start")
        if step == min(1, size - 2):
            for which in (1, 0):
                seq_copy(which, seq, far, 1).wait_recv()
                seq_copy(which, far, core, 2).start()

    gathered = jnp.zeros((8, width), f32)
    small_width = smalls.shape[2]
    for at in range(size):
        held = smalls[at].astype(f32)[0:8, :]
        lane = lax.broadcasted_iota(jnp.int32, held.shape, 1)
        wide = jnp.concatenate(
            [
                jnp.where(lane < depth, held, 0.0),
                jnp.zeros((8, width - small_width), f32),
            ],
            axis=1,
        )
        gathered += pltpu.roll(wide, at * depth, 1) if at else wide
        bias[:, at * bias_share : (at + 1) * bias_share] = held[:, :bias_share]
    gains[...] = gathered
    gain_one = gathered[0:1, :]
    gain_two = gathered[1:2, :]
    store(gains, gains_out)
    for which in (1, 0):
        seq_copy(which, seq, core, 0).wait_recv()
        seq_copy(which, far, core, 2).wait_recv()
    store(pieces, piece_out)
    store(trig_all, trig_out)

    width_query = count * HEAD_DIM * 4
    kv_lane = pl.multiple_of(width_query + (seq // 2) * HEAD_DIM, HEAD_DIM)
    value_lane = pl.multiple_of(kv_lane + KV_HEADS * HEAD_DIM, HEAD_DIM)
    own_bias = jnp.concatenate(
        [
            bias[2:3, pl.ds(pl.multiple_of(seq * own, HEAD_DIM), own)],
            bias[2:3, pl.ds(kv_lane, HEAD_DIM)],
            bias[2:3, pl.ds(value_lane, HEAD_DIM)],
        ],
        axis=1,
    )
    for at in range(length // block):
        span = slice(at * block, (at + 1) * block)
        rows = rows_all[at].astype(f32)
        normed[span, :] = (rows * inverse_of(rows) * gain_one).astype(bf16)
        mixed = matmul(normed[span, :], pieces[:, :used], NN) + own_bias
        cosine, sine = turn_tables(trig_all[at])
        for head in range(count + 1):
            turned = mixed[:, head_columns(head)]
            heads[span, head_columns(head)] = (
                turned * cosine + pltpu.roll(turned, HEAD_DIM // 2, 1) * sine
            ).astype(bf16)
        heads[span, head_columns(count + 1)] = mixed[:, head_columns(count + 1)].astype(bf16)
        if 2 * (at + 1) == length // block:
            cot_pump(1)
    store(normed, normed_out)
    store(heads, heads_out)

    for peer in (core, far, diagonal):
        for at in range(per_group):
            for side in range(2):
                pltpu.make_async_remote_copy(
                    src_ref=pieces.at[pl.ds(0, half), pl.ds(used, own)],
                    dst_ref=proj.at[pl.ds(0, half), pl.ds(0, own)],
                    send_sem=proj_send.at[side, 0],
                    recv_sem=proj_recv.at[peer, at, side],
                    device_id={"seq": peer},
                    device_id_type=MESH,
                ).wait_recv()
    for step in range(size):
        for side in range(2):
            proj_act(step, side, "wait")
    store(proj, proj_out)

    lane = lax.broadcasted_iota(jnp.int32, (block, HEAD_DIM), 1)
    for start in range(0, length, block):
        span = slice(start, start + block)
        seen = slice(0, start + block)
        logs[span, :] = jnp.zeros((block, HEAD_DIM), f32)

        @pl.loop(0, count)
        def _(at):
            head = pl.ds(pl.multiple_of(at * HEAD_DIM, HEAD_DIM), HEAD_DIM)
            scores = causal(
                matmul(heads[span, head], heads[seen, head_columns(count)], NT) * scale, start
            )
            top = jnp.max(scores, axis=-1, keepdims=True)
            exponent = jnp.exp(scores - top)
            total = jnp.sum(exponent, axis=-1, keepdims=True)
            probability = (exponent / total).astype(bf16)
            attended[span, head] = matmul(
                probability, heads[seen, head_columns(count + 1)], NN
            ).astype(bf16)
            logs[span, :] = jnp.where(lane == at, top + jnp.log(total), logs[span, :])

        if 2 * (start + block) == length:
            cot_pump(2)
    store(attended, attended_out)
    store(logs, log_out)

    def out_part(span):
        part[:, span] = matmul(attended[...], proj[:, span], NN).astype(bf16)

    for_blocks(width, 512, out_part)

    def part_rows(at):
        return part.at[pl.ds(pl.multiple_of(at * tokens, tokens), tokens)]

    to_core = [
        remote(part_rows(diagonal), seq_in.at[0], sum_sems, (0,), {"seq": core}),
        remote(part_rows(core), seq_in.at[1], sum_sems, (1,), {"seq": core}),
    ]
    to_far = remote(far_sum, seq_in.at[2], sum_sems, (2,), {"seq": far})
    for copy in to_core:
        copy.start()
    cot_pump(3)
    to_core[0].wait_recv()
    far_sum[...] = (part_rows(far)[...].astype(f32) + seq_in[0].astype(f32)).astype(bf16)
    to_far.start()
    to_core[1].wait_recv()
    resid[...] = (
        part_rows(seq)[...].astype(f32) + seq_in[1].astype(f32) + rows_all[seq].astype(f32)
    )
    cot_pump(4)
    cot_pump(5)
    to_far.wait_recv()
    resid[...] += seq_in[2].astype(f32)
    store(resid, resid_out)
    normed_two[...] = (resid[...] * inverse_of(resid[...]) * gain_two).astype(bf16)
    store(normed_two, normed_two_out)
    for step in range(6, size):
        cot_pump(step)
    for step in range(size):
        for side in range(2):
            cot_store(step, side).wait()

    for step in range(size - 1):
        for side in range(2):
            for sub in range(2):
                ring_copy(step, side, sub).wait_send()
                cot_copy(step, side, sub).wait_send()
        small_copy(step).wait_send()
    for which in (1, 0):
        seq_copy(which, seq, core, 0).wait_send()
        seq_copy(which, seq, far, 1).wait_send()
        seq_copy(which, far, core, 2).wait_send()
    for copy in to_core + [to_far]:
        copy.wait_send()
    for copy in stores:
        copy.wait()


def attend_group(rows, trig, piece, small, cots, bias_share):
    size = lax.axis_size("fsdp")
    groups = lax.axis_size("seq")
    tokens, width = rows.shape
    depth, joint = piece.shape
    own = width // groups
    used = joint - own
    length = tokens * groups
    f32, bf16 = jnp.float32, jnp.bfloat16
    dma = pltpu.SemaphoreType.DMA
    anywhere = pl.BlockSpec(memory_space=pl.ANY)
    normed = ((length, width), bf16)
    heads = ((length, used), bf16)
    attended = ((length, own), bf16)
    logs = ((length, HEAD_DIM), f32)
    pieces = ((width, joint), bf16)
    proj = ((own, width), bf16)
    trig_all = ((groups,) + trig.shape, f32)
    gains = ((8, width), f32)
    rows_all = ((groups, tokens, width), bf16)
    own_rows = ((tokens, width), bf16)
    resid = ((tokens, width), f32)
    cots_all = ((size, tokens, width), bf16)
    outs = (
        normed, heads, attended, logs, pieces, proj, trig_all, gains, own_rows, resid, cots_all
    )
    held = (
        rows_all,
        trig_all,
        pieces,
        proj,
        ((size,) + small.shape, bf16),
        cots_all,
        normed,
        heads,
        attended,
        logs,
        normed,
        gains,
        ((8, size * bias_share), f32),
        resid,
        ((3, tokens, width), bf16),
        own_rows,
        own_rows,
    )
    return pl.pallas_call(
        functools.partial(attend_forward_kernel, size, tokens, bias_share),
        out_shape=tuple(jax.ShapeDtypeStruct(*shape) for shape in outs),
        in_specs=[anywhere] * 5,
        out_specs=(anywhere,) * len(outs),
        scratch_shapes=[pltpu.VMEM(*shape) for shape in held]
        + [
            dma((5,)),
            dma((len(outs),)),
            dma((2, 2, 2, size)),
            dma((2, size)),
            dma((2, 2, 2, size)),
            dma((2, size)),
            dma((2, 2, 3)),
            dma((2, 3)),
            dma((2, size)),
            dma((groups, own // depth, 2)),
        ],
        compiler_params=pltpu.CompilerParams(
            collective_id=1, has_side_effects=True, vmem_limit_bytes=VMEM_BYTES
        ),
        name="attend_forward",
    )(rows, trig, piece, small, cots)


CHUNKS = 5
IN_LOOP = ((2, 1), (4, 2), (6, 3))


def mlp_kernel(
    size,
    normed_ref,
    resid_ref,
    gain_ref,
    cots_ref,
    gate_ref,
    up_ref,
    down_ref,
    outs_ref,
    back_ref,
    gain_grad_ref,
    sums_ref,
    far_ref,
    rows_all,
    cots,
    weights,
    grads,
    hid,
    dgate,
    dup,
    resid,
    sums_in,
    backs,
    outs,
    load_sems,
    cot_sems,
    ring_send,
    ring_recv,
    sum_send,
    sum_recv,
    out_sems,
    swap_sems,
    far_sems,
    swap_ready,
):
    tokens, width = normed_ref.shape
    units = gate_ref.shape[0]
    half = tokens // 2
    me = lax.axis_index("fsdp")
    seq = lax.axis_index("seq")
    place = ring_place(me, size)
    right = ring_member((place + 1) % size, size)
    left = ring_member((place + size - 1) % size, size)
    core, far, diagonal = seq_partners(seq)
    sides = ((right, pl.ds(0, half)), (left, pl.ds(half, half)))

    def owner_of(step, side):
        return ring_member((place + size - step if side == 0 else place + step) % size, size)

    own_load = pltpu.make_async_copy(normed_ref, rows_all.at[0], load_sems.at[3])
    resid_load = pltpu.make_async_copy(resid_ref, resid, load_sems.at[4])
    weight_loads = [
        pltpu.make_async_copy(ref, weights.at[at], load_sems.at[at])
        for at, ref in enumerate((gate_ref, up_ref, down_ref))
    ]
    own_load.start()
    greet(({"fsdp": right}, {"fsdp": left}, {"seq": core}, {"seq": far}))

    def cot_copies(step):
        return [
            pltpu.make_async_copy(
                cots_ref.at[
                    pl.ds(
                        pl.multiple_of(owner_of(step, side) * tokens + side * half, half), half
                    )
                ],
                cots.at[step % 2, sides[side][1]],
                cot_sems.at[step % 2, side],
            )
            for side in range(2)
        ]


    def row_copy(step, side):
        target, span = sides[side]
        return pltpu.make_async_remote_copy(
            src_ref=rows_all.at[step, span],
            dst_ref=rows_all.at[step + 1, span],
            send_sem=ring_send.at[side, step],
            recv_sem=ring_recv.at[side, step + 1],
            device_id={"fsdp": target},
            device_id_type=MESH,
        )

    def sum_span(side, sub):
        return pl.ds(side * half + sub * (half // 2), half // 2)

    def sum_copy(step, side, sub):
        target, span = sides[side][0], sum_span(side, sub)
        return pltpu.make_async_remote_copy(
            src_ref=backs.at[step, span],
            dst_ref=sums_in.at[step, span],
            send_sem=sum_send.at[side, sub, step],
            recv_sem=sum_recv.at[side, sub, step],
            device_id={"fsdp": target},
            device_id_type=MESH,
        )

    def sum_step(step):
        for sub in range(2):
            for side in range(2):
                span = sum_span(side, sub)
                if step >= 2:
                    sum_copy(step - 1, side, sub).wait_recv()
                    backs[step, span] = (
                        backs[step, span].astype(jnp.float32)
                        + sums_in[step - 1, span].astype(jnp.float32)
                    ).astype(jnp.bfloat16)
                sum_copy(step, side, sub).start()

    def out_copy(step, side):
        at = pl.multiple_of(owner_of(step, side) * tokens + side * half, half)
        return pltpu.make_async_copy(
            outs.at[step % 2, sides[side][1]], outs_ref.at[pl.ds(at, half)], out_sems.at[side, step]
        )

    def elementwise(step, span):
        rows = rows_all[step]
        gate = matmul(rows, weights[0, span, :], NT)
        up = matmul(rows, weights[1, span, :], NT)
        grad_hidden = matmul(cots[step % 2], weights[2, span, :], NT)
        sigmoid = jax.nn.sigmoid(gate)
        activated = gate * sigmoid
        hid[:, span] = (activated * up).astype(jnp.bfloat16)
        dgate[:, span] = (
            grad_hidden * up * sigmoid * (1.0 + gate * (1.0 - sigmoid))
        ).astype(jnp.bfloat16)
        dup[:, span] = (grad_hidden * activated).astype(jnp.bfloat16)

    own_load.wait()
    for side in range(2):
        row_copy(0, side).start()
    for load in weight_loads + cot_copies(0) + [resid_load]:
        load.start()

    @pl.loop(0, units // 16)
    def _(at):
        zeros = jnp.zeros((3, 16, width), jnp.float32)
        grads[:, pl.ds(pl.multiple_of(at * 16, 16), 16), :] = zeros

    for load in weight_loads:
        load.wait()

    @pl.loop(0, size)
    def _(step):
        slot = step % 2

        @pl.when(step >= 1)
        def _():
            for side in range(2):
                row_copy(step - 1, side).wait_recv()

        @pl.when((step >= 1) & (step < size - 1))
        def _():
            for side in range(2):
                row_copy(step, side).start()

        for load in cot_copies(step):
            load.wait()

        @pl.when(step < size - 1)
        def _():
            for load in cot_copies(step + 1):
                load.start()

        for_blocks(units, 256, functools.partial(elementwise, step))

        def back_part(span):
            backs[step, :, span] = (
                matmul(dgate[...], weights[0, :, span], NN)
                + matmul(dup[...], weights[1, :, span], NN)
            ).astype(jnp.bfloat16)

        for_blocks(width, 256, back_part)

        for when, at in IN_LOOP:

            @pl.when(step == when)
            def _():
                sum_step(at)

        @pl.when(step >= 2)
        def _():
            for side in range(2):
                out_copy(step - 2, side).wait()

        def out_part(span):
            outs[slot, :, span] = matmul(hid[...], weights[2, :, span], NN).astype(jnp.bfloat16)

        for_blocks(width, 256, out_part)
        for side in range(2):
            out_copy(step, side).start()

        def weight_part(span):
            rows, cot = rows_all[step, :, span], cots[slot, :, span]
            grads[0, :, span] += matmul(dgate[...], rows, TN)
            grads[1, :, span] += matmul(dup[...], rows, TN)
            grads[2, :, span] += matmul(hid[...], cot, TN)

        for_blocks(width, 256, weight_part)

    share = units // 2
    kept = pl.multiple_of((seq % 2) * share, 16)
    given = pl.multiple_of((1 - seq % 2) * share, 16)
    chunk = share // CHUNKS
    pl.semaphore_signal(swap_ready, inc=1, device_id={"seq": core}, device_id_type=MESH)

    def to_seq(source, target, sems, at, device):
        return pltpu.make_async_remote_copy(
            src_ref=source,
            dst_ref=target,
            send_sem=sems.at[0, at],
            recv_sem=sems.at[1, at],
            device_id={"seq": device},
            device_id_type=MESH,
        )

    swaps = [
        to_seq(
            weights.at[at, pl.ds(given, share)],
            weights.at[at, pl.ds(given, share)],
            swap_sems,
            at,
            core,
        )
        for at in range(3)
    ]
    waiting = [at for at in range(1, size) if at not in [pair[1] for pair in IN_LOOP]]
    sum_step(waiting[0])
    for at in range(3):

        @pl.loop(0, share // 16)
        def _(block):
            span = pl.ds(pl.multiple_of(given + block * 16, 16), 16)
            weights[at, span, :] = grads[at, span, :].astype(jnp.bfloat16)

        if at == 0:
            pl.semaphore_wait(swap_ready, 1)
        swaps[at].start()

    stores = []

    def kept_rows(at):
        return pl.ds(pl.multiple_of(kept + at * chunk, 16), chunk)

    far_copies = [
        to_seq(weights.at[0, kept_rows(at)], far_ref.at[kept_rows(at)], far_sems, at, far)
        for at in range(CHUNKS)
    ]
    def swap_finish(at):
        swaps[at].wait_recv()

        @pl.loop(0, share // 16)
        def _(block):
            span = pl.ds(pl.multiple_of(kept + block * 16, 16), 16)
            weights[at, span, :] = (
                grads[at, span, :] + weights[at, span, :].astype(jnp.float32)
            ).astype(jnp.bfloat16)

        done = weights.at[at, pl.ds(kept, share)]
        stores.append(
            pltpu.make_async_copy(done, sums_ref.at[at, pl.ds(kept, share)], load_sems.at[at])
        )
        if at == 0:
            for copy in far_copies:
                copy.start()
        stores[-1].start()

    cot_own = pltpu.make_async_copy(
        cots_ref.at[pl.ds(pl.multiple_of(me * tokens, tokens), tokens)],
        cots.at[0],
        load_sems.at[7],
    )
    cot_own.start()
    for turn, at in enumerate(waiting[1:]):
        sum_step(at)
        if turn < 3:
            swap_finish(turn)
    for turn in range(len(waiting) - 1, 3):
        swap_finish(turn)

    for side in range(2):
        for sub in range(2):
            sum_copy(size - 1, side, sub).wait_recv()
    grad_normed = backs[0].astype(jnp.float32) + sums_in[size - 1].astype(jnp.float32)
    resid_load.wait()
    inverse = inverse_of(resid[...])
    unit_rows = resid[...] * inverse
    gain_grad_ref[...] = jnp.sum(grad_normed * unit_rows, axis=0, keepdims=True)
    grad_unit = grad_normed * gain_ref[...]
    cot_own.wait()
    back_ref[...] = cots[0].astype(jnp.float32) + inverse * (
        grad_unit - unit_rows * jnp.mean(grad_unit * unit_rows, axis=-1, keepdims=True)
    )
    for side in range(2):
        out_copy(size - 2, side).wait()
        out_copy(size - 1, side).wait()

        @pl.loop(0, size - 1)
        def _(step):
            row_copy(step, side).wait_send()
            for sub in range(2):
                sum_copy(step + 1, side, sub).wait_send()

    for copy in swaps + far_copies:
        copy.wait_send()
    for copy in far_copies:
        copy.wait_recv()
    for store in stores:
        store.wait()


def mlp_ring(normed, resid, gain, cots, gate_weight, up_weight, down_weight):
    size = lax.axis_size("fsdp")
    tokens, width = normed.shape
    units = gate_weight.shape[0]
    anywhere = pl.BlockSpec(memory_space=pl.ANY)
    inside = pl.BlockSpec(memory_space=pltpu.VMEM)
    bf16, f32 = jnp.bfloat16, jnp.float32
    dma = pltpu.SemaphoreType.DMA
    return pl.pallas_call(
        functools.partial(mlp_kernel, size),
        out_shape=(
            jax.ShapeDtypeStruct((size * tokens, width), bf16),
            jax.ShapeDtypeStruct((tokens, width), f32),
            jax.ShapeDtypeStruct((1, width), f32),
            jax.ShapeDtypeStruct((3, units, width), bf16),
            jax.ShapeDtypeStruct((units, width), bf16),
        ),
        in_specs=[anywhere, anywhere, inside, anywhere, anywhere, anywhere, anywhere],
        out_specs=(anywhere, inside, inside, anywhere, anywhere),
        scratch_shapes=[
            pltpu.VMEM((size, tokens, width), bf16),
            pltpu.VMEM((2, tokens, width), bf16),
            pltpu.VMEM((3, units, width), bf16),
            pltpu.VMEM((3, units, width), f32),
            pltpu.VMEM((tokens, units), bf16),
            pltpu.VMEM((tokens, units), bf16),
            pltpu.VMEM((tokens, units), bf16),
            pltpu.VMEM((tokens, width), f32),
            pltpu.VMEM((size, tokens, width), bf16),
            pltpu.VMEM((size, tokens, width), bf16),
            pltpu.VMEM((2, tokens, width), bf16),
            dma((9,)),
            dma((2, 2)),
            dma((2, size)),
            dma((2, size)),
            dma((2, 2, size)),
            dma((2, 2, size)),
            dma((2, size)),
            dma((2, 3)),
            dma((2, CHUNKS)),
            pltpu.SemaphoreType.REGULAR,
        ],
        compiler_params=pltpu.CompilerParams(
            collective_id=0, has_side_effects=True, vmem_limit_bytes=VMEM_BYTES
        ),
        name="mlp_ring",
    )(normed, resid, gain, cots, gate_weight, up_weight, down_weight)


def attend_backward_kernel(
    size,
    heads_ref,
    attended_ref,
    log_ref,
    proj_ref,
    weight_ref,
    normed_ref,
    trig_ref,
    hidden_ref,
    resid_grad_ref,
    gain_ref,
    gain_grad_ref,
    resid_ref,
    outs_ref,
    units_in_ref,
    far_gate_in_ref,
    grad_in_ref,
    hidden_out_ref,
    small_ref,
    shards_ref,
    halves_ref,
    far_units_ref,
    units_ref,
    far_gate_ref,
    grads_all,
    grad_heads,
    grad_mixed,
    grad_keys,
    grad_values,
    grad_normed,
    term_qkv,
    term_out,
    out_columns,
    qkv_in,
    out_in,
    qkv_sum,
    out_sum,
    shard,
    shard_all,
    half_shard,
    half_all,
    out_own,
    out_recv,
    out_send,
    resid,
    seq_in,
    far_sum,
    small_in,
    load_sems,
    own_sems,
    out_sems,
    term_sems,
    column_sems,
    seq_sems,
    shard_sems,
    small_sems,
    unit_sems,
    pass_sems,
    share_sems,
    gate_sems,
    grad_sems,
):
    length = heads_ref.shape[0]
    tokens, width = hidden_ref.shape
    used = heads_ref.shape[1]
    own = attended_ref.shape[1]
    count = own // HEAD_DIM
    scale = HEAD_DIM**-0.5
    half = tokens // 2
    block = tokens
    depth = width // size
    chip_pieces = size // 2
    half_width = width // 2
    term_half = depth // 2
    units = units_ref.shape[1]
    f32, bf16 = jnp.float32, jnp.bfloat16
    me = lax.axis_index("fsdp")
    seq = lax.axis_index("seq")
    place = ring_place(me, size)
    right = ring_member((place + 1) % size, size)
    left = ring_member((place + size - 1) % size, size)
    core, far, diagonal = seq_partners(seq)
    rounds = size.bit_length() - 1
    mirrors = [me + (1 - 2 * ((me // 2**at) % 2)) * 2**at for at in range(rounds)]
    ring = ({"fsdp": right}, {"fsdp": left})

    def owner_of(step, side):
        return ring_member((place + size - step if side == 0 else place + step) % size, size)

    def remote(source, target, sems, at, device):
        return pltpu.make_async_remote_copy(
            src_ref=source,
            dst_ref=target,
            send_sem=sems.at[(0,) + at],
            recv_sem=sems.at[(1,) + at],
            device_id=device,
            device_id_type=MESH,
        )

    greet(
        ring
        + ({"seq": core}, {"seq": far})
        + tuple({"fsdp": mirror} for mirror in mirrors)
    )

    def own_load(step, side):
        at = pl.multiple_of(owner_of(step, side) * tokens + side * half, half)
        return pltpu.make_async_copy(
            outs_ref.at[pl.ds(at, half)],
            out_own.at[step % 2, pl.ds(side * half, half)],
            own_sems.at[step % 2, side],
        )

    def out_copy(step, side):
        span = pl.ds(side * half, half)
        return remote(
            out_send.at[step % 2, span], out_recv.at[step, span], out_sems, (side, step), ring[side]
        )

    def out_step(step):
        for side in range(2):
            own_load(step, side).wait()
            if step < size - 1:
                own_load(step + 1, side).start()
            if step >= 3:
                out_copy(step - 2, side).wait_send()
            if step >= 2:
                out_copy(step - 1, side).wait_recv()
        total = out_own[step % 2].astype(f32)
        if step >= 2:
            total += out_recv[step - 1].astype(f32)
        out_send[step % 2] = total.astype(bf16)
        for side in range(2):
            out_copy(step, side).start()

    resid_load = pltpu.make_async_copy(resid_ref, resid, load_sems.at[0])

    def out_finish():
        step = size
        for side in range(2):
            out_copy(step - 2, side).wait_send()
            out_copy(step - 1, side).wait_send()
            out_copy(step - 1, side).wait_recv()
        mine = pltpu.make_async_copy(
            outs_ref.at[pl.ds(pl.multiple_of(me * tokens, tokens), tokens)],
            out_own.at[0],
            load_sems.at[1],
        )
        mine.start()
        mine.wait()
        resid_load.wait()
        hidden_out_ref[...] = (
            resid[...] + out_own[0].astype(f32) + out_recv[size - 1].astype(f32)
        ).astype(bf16)

    share = units // 2
    piece = share // CHUNKS
    kept = (seq % 2) * share

    def unit_slice(ref, at):
        start = pl.multiple_of(kept + (at % CHUNKS) * piece, 16)
        return ref.at[at // CHUNKS, pl.ds(start, piece)]

    def unit_copy(at):
        return remote(
            unit_slice(units_ref, at + CHUNKS), unit_slice(far_units_ref, at), unit_sems, (at,), {"seq": far}
        )

    def unit_pass(at):
        part = unit_slice(far_units_ref, at)
        return remote(part, part, pass_sems, (at,), {"seq": core})

    def unit_share(at):
        part = unit_slice(units_ref, at)
        return remote(part, part, share_sems, (at,), {"seq": core})

    def gate_pass(at):
        part = far_gate_ref.at[pl.ds(pl.multiple_of(kept + at * piece, 16), piece)]
        return remote(part, part, gate_sems, (at,), {"seq": core})

    chunks = 2 * CHUNKS
    starts, passes = iter(range(chunks)), iter(range(chunks))

    def send_units(number):
        for _ in range(number):
            unit_copy(next(starts)).start()

    def pass_units(number):
        for _ in range(number):
            at = next(passes)
            unit_copy(at).wait_recv()
            unit_pass(at).start()

    def grad_copy(source, target, at):
        span = grads_all.at[source]
        return remote(span, span, grad_sems, (at,), {"seq": target})

    to_far_grads = grad_copy(seq, far, 0)
    to_core_grads = grad_copy(seq, core, 1)
    passed_grads = grad_copy(far, core, 2)
    grads_all[seq] = resid_grad_ref[...].astype(bf16)
    to_far_grads.start()
    to_core_grads.start()
    resid_load.start()
    for side in range(2):
        own_load(1, side).start()
    out_step(1)

    grad_keys[...] = jnp.zeros_like(grad_keys)
    grad_values[...] = jnp.zeros_like(grad_values)
    lane = lax.broadcasted_iota(jnp.int32, (block, HEAD_DIM), 1)
    keys = slice(own, own + HEAD_DIM)
    values = slice(own + HEAD_DIM, used)

    def attend_block(at_block):
        start = at_block * block
        span = slice(start, start + block)
        seen = slice(0, start + block)
        cosine, sine = turn_tables(trig_ref[span, :])
        grad_heads[span, :] = matmul(grads_all[at_block], proj_ref[...], NT).astype(bf16)

        @pl.loop(0, count)
        def _(at):
            head = pl.ds(pl.multiple_of(at * HEAD_DIM, HEAD_DIM), HEAD_DIM)
            query = heads_ref[span, head]
            grad = grad_heads[span, head]
            logs = jnp.sum(jnp.where(lane == at, log_ref[span, :], 0.0), axis=-1, keepdims=True)
            scores = causal(matmul(query, heads_ref[seen, keys], NT) * scale, start)
            probability = jnp.exp(scores - logs)
            grad_probs = matmul(grad, heads_ref[seen, values], NT)
            delta = jnp.sum(probability * grad_probs, axis=-1, keepdims=True)
            grad_scores = (probability * (grad_probs - delta)).astype(bf16)
            grad_query = matmul(grad_scores, heads_ref[seen, keys], NN) * scale
            grad_query = grad_query.astype(bf16).astype(f32)
            grad_mixed[span, head] = (
                grad_query * cosine + pltpu.roll(grad_query * sine, HEAD_DIM // 2, 1)
            ).astype(bf16)
            grad_keys[seen, :] += matmul(grad_scores, query, TN) * scale
            grad_values[seen, :] += matmul(probability.astype(bf16), grad, TN)

    @pl.loop(0, 4)
    def _(turn):
        @pl.when(turn == 1)
        def _():
            to_core_grads.wait_recv()

        @pl.when(turn == 2)
        def _():
            to_far_grads.wait_recv()
            passed_grads.start()
            unit_copy(0).start()

        @pl.when(turn == 3)
        def _():
            passed_grads.wait_recv()
            unit_copy(1).start()

        @pl.when(turn == 2)
        def _():
            out_step(2)

        for shared in range(3):
            unit_share(turn * 3 + shared).start()
        gate_pass(turn).start()
        at_block = ((seq // 2 + turn // 2) % 2) * 2 + (seq % 2 + turn % 2) % 2
        for at in range(4):

            @pl.when(at_block == at)
            def _():
                attend_block(at)

    next(starts)
    next(starts)
    send_units(1)
    for shared in range(12, 3 * CHUNKS):
        unit_share(shared).start()
    gate_pass(4).start()
    out_step(3)

    for start in range(0, length, block):
        span = slice(start, start + block)
        cosine, sine = turn_tables(trig_ref[span, :])
        part = grad_keys[span, :].astype(bf16).astype(f32)
        grad_mixed[span, keys] = (
            part * cosine + pltpu.roll(part * sine, HEAD_DIM // 2, 1)
        ).astype(bf16)
        grad_mixed[span, values] = grad_values[span, :].astype(bf16)

    def normed_part(span):
        grad_normed[:, span] = matmul(grad_mixed[...], weight_ref[span, :used], NT).astype(bf16)

    loop_blocks(width, 256, normed_part)

    def block_rows(at):
        return grad_normed.at[pl.ds(pl.multiple_of(at * tokens, tokens), tokens)]

    to_core = [
        remote(block_rows(diagonal), seq_in.at[0], seq_sems, (0,), {"seq": core}),
        remote(block_rows(core), seq_in.at[1], seq_sems, (1,), {"seq": core}),
    ]
    to_far = remote(far_sum, seq_in.at[2], seq_sems, (2,), {"seq": far})
    for copy in to_core:
        copy.start()

    def out_term(span):
        term_out[:, span] = matmul(
            attended_ref[...], grads_all[:, :, span].reshape(length, span.size), TN
        ).astype(bf16)

    loop_blocks(width, 256, out_term)
    my_row = pl.multiple_of((seq % 2) * own, 16)
    my_lane = pl.multiple_of((seq % 2) * half_width, 128)
    core_lane = pl.multiple_of((1 - seq % 2) * half_width, 128)
    columns = remote(
        term_out.at[:, pl.ds(core_lane, half_width)],
        out_columns.at[pl.ds(my_row, own)],
        column_sems,
        (0,),
        {"seq": core},
    )
    columns.start()
    out_columns[pl.ds(my_row, own), :] = term_out[:, pl.ds(my_lane, half_width)]

    def qkv_term(span):
        term_qkv[span, :] = matmul(normed_ref[:, span], grad_mixed[...], TN).astype(bf16)

    loop_blocks(width, 256, qkv_term)
    to_core[0].wait_recv()
    far_sum[...] = (block_rows(far)[...].astype(f32) + seq_in[0].astype(f32)).astype(bf16)
    to_far.start()
    out_step(4)
    small_in[0] = jnp.zeros((8, width), f32)
    small_in[0, 1:2, :] = gain_grad_ref[...]
    bias = jnp.sum(grad_mixed[...].astype(f32), axis=0, keepdims=True)
    small_in[0, 2:3, pl.ds(pl.multiple_of(seq * own, 128), own)] = bias[:, :own]
    kv_lane = pl.multiple_of((seq // 2) * HEAD_DIM, HEAD_DIM)
    small_in[0, 3:4, pl.ds(kv_lane, HEAD_DIM)] = bias[:, keys]
    small_in[0, 3:4, pl.ds(kv_lane + KV_HEADS * HEAD_DIM, HEAD_DIM)] = bias[:, values]

    def term_copy(step, side):
        span = pl.ds(side * term_half, term_half)
        return remote(
            qkv_sum.at[step, span], qkv_in.at[step, span], term_sems, (0, side, step), ring[side]
        )

    def half_copy(step, side):
        span = pl.ds(side * term_half, term_half)
        return remote(
            out_sum.at[step, span], out_in.at[step, span], term_sems, (1, side, step), ring[side]
        )

    def here(owner):
        return owner // chip_pieces == seq // 2

    def half_rows(owner, side):
        start = (owner % chip_pieces) * depth + side * term_half
        return pl.ds(pl.multiple_of(start, 16), term_half)

    def term_step(step):
        for side in range(2):
            span = pl.ds(side * term_half, term_half)
            start = owner_of(step, side) * depth + side * term_half
            total = term_qkv[pl.ds(pl.multiple_of(start, 16), term_half), :].astype(f32)
            if step >= 2:
                term_copy(step - 1, side).wait_recv()
                total += qkv_in[step - 1, span, :].astype(f32)
            qkv_sum[step, span, :] = total.astype(bf16)
            term_copy(step, side).start()

    def half_step(step):
        for side in range(2):
            owner = owner_of(step, side)

            @pl.when(here(owner))
            def _():
                span = pl.ds(side * term_half, term_half)
                total = out_columns[half_rows(owner, side), :].astype(f32)
                if step >= 2:
                    half_copy(step - 1, side).wait_recv()
                    total += out_in[step - 1, span, :].astype(f32)
                out_sum[step, span, :] = total.astype(bf16)
                half_copy(step, side).start()

    def small_copy(at):
        device = ({"seq": core}, {"seq": far})[at] if at < 2 else {"fsdp": mirrors[at - 2]}
        return remote(small_in.at[2 * at], small_in.at[2 * at + 1], small_sems, (at,), device)

    def small_step(at):
        small_copy(at).wait_recv()
        small_in[2 * at + 2] = small_in[2 * at] + small_in[2 * at + 1]

    term_step(1)
    columns.wait_recv()
    half_step(1)
    term_step(2)
    half_step(2)
    out_step(5)
    to_core[1].wait_recv()
    to_far.wait_recv()
    rows = hidden_ref[...].astype(f32)
    inverse = lax.rsqrt(jnp.mean(rows * rows, axis=-1, keepdims=True) + norm_eps)
    unit_rows = rows * inverse
    grad_rows = (
        block_rows(seq)[...].astype(f32) + seq_in[1].astype(f32) + seq_in[2].astype(f32)
    )
    small_in[0, 0:1, :] = jnp.sum(grad_rows * unit_rows, axis=0, keepdims=True)
    small_copy(0).start()
    grad_unit = grad_rows * gain_ref[...]
    grad_in_ref[...] = resid_grad_ref[...] + inverse * (
        grad_unit - unit_rows * jnp.mean(grad_unit * unit_rows, axis=-1, keepdims=True)
    )
    total_rounds = rounds + 2
    small_step(0)
    small_copy(1).start()
    done = 1
    send_units(3)
    for step in range(3, size):
        term_step(step)
        half_step(step)
        if done < total_rounds:
            small_step(done)
            done += 1
            if done < total_rounds:
                small_copy(done).start()
        if step == 4:
            send_units(2)
        if step % 2 == 0:
            pass_units(2)
    while done < total_rounds:
        small_step(done)
        done += 1
        if done < total_rounds:
            small_copy(done).start()
    small_ref[...] = small_in[2 * total_rounds]
    source_chip = here(me)
    for side in range(2):
        span = pl.ds(side * term_half, term_half)
        start = me * depth + side * term_half
        term_copy(size - 1, side).wait_recv()
        shard[span, :] = (
            term_qkv[pl.ds(pl.multiple_of(start, 16), term_half), :].astype(f32)
            + qkv_in[size - 1, span, :].astype(f32)
        ).astype(bf16)

        @pl.when(source_chip)
        def _():
            half_copy(size - 1, side).wait_recv()
            half_shard[span, :] = (
                out_columns[half_rows(me, side), :].astype(f32)
                + out_in[size - 1, span, :].astype(f32)
            ).astype(bf16)

    def shard_copy(source, at, block_at, target):
        return remote(source, shard_all.at[block_at], shard_sems, (at,), {"seq": target})

    def half_move(source, at, target):
        return remote(source, half_all.at[seq % 2], shard_sems, (at,), {"seq": target})

    shard_far = shard_copy(shard, 0, seq, far)
    shard_core = shard_copy(shard, 1, seq, core)
    shard_pass = shard_copy(shard_all.at[far], 2, far, core)
    half_far = half_move(half_shard, 3, far)
    half_core = half_move(half_shard, 4, core)
    half_pass = half_move(half_all.at[seq % 2], 5, core)
    shard_far.start()
    shard_core.start()

    @pl.when(source_chip)
    def _():
        half_far.start()
        half_core.start()
        half_all[seq % 2] = half_shard[...]

    send_units(2)
    shard_all[seq] = shard[...]
    out_step(6)
    shard_far.wait_recv()
    shard_pass.start()

    @pl.when(jnp.logical_not(source_chip))
    def _():
        half_far.wait_recv()
        half_pass.start()

    pass_units(3)
    out_step(7)
    pass_units(3)
    out_finish()
    shard_core.wait_recv()
    shard_pass.wait_recv()
    shard_store = pltpu.make_async_copy(shard_all, shards_ref, load_sems.at[1])
    shard_store.start()

    @pl.when(source_chip)
    def _():
        half_core.wait_recv()
        half_core.wait_send()
        half_far.wait_send()

    @pl.when(jnp.logical_not(source_chip))
    def _():
        half_pass.wait_recv()
        half_pass.wait_send()

    half_store = pltpu.make_async_copy(half_all, halves_ref, load_sems.at[2])
    half_store.start()
    for step in range(1, size):
        for side in range(2):
            term_copy(step, side).wait_send()

            @pl.when(here(owner_of(step, side)))
            def _():
                half_copy(step, side).wait_send()

    for copy in [unit_share(at) for at in range(3 * CHUNKS)] + [
        gate_pass(at) for at in range(CHUNKS)
    ]:
        copy.wait_send()
        copy.wait_recv()
    for at in range(chunks):
        unit_pass(at).wait_recv()
        unit_copy(at).wait_send()
        unit_pass(at).wait_send()
    for at in range(total_rounds):
        small_copy(at).wait_send()
    for copy in to_core + [to_far, columns, shard_far, shard_core, shard_pass]:
        copy.wait_send()
    for copy in (to_far_grads, to_core_grads, passed_grads):
        copy.wait_send()
    shard_store.wait()
    half_store.wait()


def attend_group_backward(
    heads,
    attended,
    logs,
    proj,
    weight,
    normed,
    trig,
    hidden,
    resid_grad,
    gain,
    gain_grad,
    resid,
    outs,
    units,
    far_gate,
):
    size = lax.axis_size("fsdp")
    groups = lax.axis_size("seq")
    length = heads.shape[0]
    tokens, width = hidden.shape
    used = heads.shape[1]
    own = attended.shape[1]
    depth = width // size
    rounds = size.bit_length() + 1
    bf16, f32 = jnp.bfloat16, jnp.float32
    anywhere = pl.BlockSpec(memory_space=pl.ANY)
    inside = pl.BlockSpec(memory_space=pltpu.VMEM)
    dma = pltpu.SemaphoreType.DMA
    vmem = pltpu.VMEM
    return pl.pallas_call(
        functools.partial(attend_backward_kernel, size),
        out_shape=(
            jax.ShapeDtypeStruct((tokens, width), f32),
            jax.ShapeDtypeStruct((tokens, width), bf16),
            jax.ShapeDtypeStruct((8, width), f32),
            jax.ShapeDtypeStruct((groups, depth, used), bf16),
            jax.ShapeDtypeStruct((2, depth, width // 2), bf16),
            jax.ShapeDtypeStruct((2,) + units.shape[1:], bf16),
            jax.ShapeDtypeStruct(units.shape, bf16),
            jax.ShapeDtypeStruct(far_gate.shape, bf16),
        ),
        in_specs=[inside] * 11 + [anywhere] * 4,
        out_specs=(inside, inside, inside) + (anywhere,) * 5,
        input_output_aliases={13: 6, 14: 7},
        scratch_shapes=[
            vmem((groups, tokens, width), bf16),
            vmem((length, own), bf16),
            vmem((length, used), bf16),
            vmem((length, HEAD_DIM), f32),
            vmem((length, HEAD_DIM), f32),
            vmem((length, width), bf16),
            vmem((width, used), bf16),
            vmem((own, width), bf16),
            vmem((2 * own, width // 2), bf16),
            vmem((size, depth, used), bf16),
            vmem((size, depth, width // 2), bf16),
            vmem((size, depth, used), bf16),
            vmem((size, depth, width // 2), bf16),
            vmem((depth, used), bf16),
            vmem((groups, depth, used), bf16),
            vmem((depth, width // 2), bf16),
            vmem((2, depth, width // 2), bf16),
            vmem((2, tokens, width), bf16),
            vmem((size, tokens, width), bf16),
            vmem((2, tokens, width), bf16),
            vmem((tokens, width), f32),
            vmem((3, tokens, width), bf16),
            vmem((tokens, width), bf16),
            vmem((2 * rounds + 1, 8, width), f32),
            dma((3,)),
            dma((2, 2)),
            dma((2, 2, size)),
            dma((2, 2, 2, size)),
            dma((2, 1)),
            dma((2, 3)),
            dma((2, 6)),
            dma((2, rounds)),
            dma((2, 2 * CHUNKS)),
            dma((2, 2 * CHUNKS)),
            dma((2, 3 * CHUNKS)),
            dma((2, CHUNKS)),
            dma((2, 3)),
        ],
        compiler_params=pltpu.CompilerParams(
            collective_id=2, has_side_effects=True, vmem_limit_bytes=VMEM_BYTES
        ),
        name="attend_backward",
    )(
        heads,
        attended,
        logs,
        proj,
        weight,
        normed,
        trig,
        hidden,
        resid_grad,
        gain,
        gain_grad,
        resid,
        outs,
        units,
        far_gate,
    )


def finish_kernel(
    sums_ref,
    far_gate_ref,
    far_ref,
    grad_in_ref,
    hidden_ref,
    shards_ref,
    halves_ref,
    gate_out,
    up_out,
    down_out,
    grad_in_out,
    hidden_out,
    qkv_out,
    proj_out,
):
    f32 = jnp.float32
    gate_out[...] = sums_ref[0].astype(f32) + far_gate_ref[...].astype(f32)
    up_out[...] = sums_ref[1].astype(f32) + far_ref[0].astype(f32)
    down_out[...] = sums_ref[2].astype(f32) + far_ref[1].astype(f32)
    grad_in_out[...] = grad_in_ref[...]
    hidden_out[...] = hidden_ref[...]
    groups, _, used = shards_ref.shape
    own = used - 2 * HEAD_DIM
    for at in range(groups):
        qkv_out[:, at * own : (at + 1) * own] = shards_ref[at, :, :own].astype(f32)
    for which in range(2):
        lanes = slice(own + which * HEAD_DIM, own + (which + 1) * HEAD_DIM)
        for head in range(KV_HEADS):
            at = groups * own + (which * KV_HEADS + head) * HEAD_DIM
            qkv_out[:, at : at + HEAD_DIM] = shards_ref[2 * head, :, lanes].astype(
                f32
            ) + shards_ref[2 * head + 1, :, lanes].astype(f32)
    half = halves_ref.shape[2]
    for which in range(2):
        proj_out[:, which * half : (which + 1) * half] = halves_ref[which].astype(f32)


def finish_totals(unit_sums, far_gate, far_sums, grad_in, hidden, shards, halves):
    f32, bf16 = jnp.float32, jnp.bfloat16
    _, units, width = unit_sums.shape
    groups, depth, used = shards.shape
    joint = groups * (used - 2 * HEAD_DIM) + 2 * KV_HEADS * HEAD_DIM
    tokens = grad_in.shape[0]
    steps, few = 10, 8

    def spec(*dims, many=False):
        lead = len(dims) - 2
        return pl.BlockSpec(
            dims,
            lambda at: (0,) * lead + (at if many else jnp.minimum(at, few - 1), 0),
        )

    rows = units // steps
    return pl.pallas_call(
        finish_kernel,
        grid=(steps,),
        out_shape=(
            jax.ShapeDtypeStruct((units, width), f32),
            jax.ShapeDtypeStruct((units, width), f32),
            jax.ShapeDtypeStruct((units, width), f32),
            jax.ShapeDtypeStruct((tokens, width), f32),
            jax.ShapeDtypeStruct((tokens, width), bf16),
            jax.ShapeDtypeStruct((depth, joint), f32),
            jax.ShapeDtypeStruct((depth, width), f32),
        ),
        in_specs=[
            spec(3, rows, width, many=True),
            spec(rows, width, many=True),
            spec(2, rows, width, many=True),
            spec(tokens // few, width),
            spec(tokens // few, width),
            spec(groups, depth // few, used),
            spec(2, depth // few, width // 2),
        ],
        out_specs=(
            spec(rows, width, many=True),
            spec(rows, width, many=True),
            spec(rows, width, many=True),
            spec(tokens // few, width),
            spec(tokens // few, width),
            spec(depth // few, joint),
            spec(depth // few, width),
        ),
        compiler_params=pltpu.CompilerParams(vmem_limit_bytes=VMEM_BYTES),
        name="finish_totals",
    )(unit_sums, far_gate, far_sums, grad_in, hidden, shards, halves)


def kernels_fit(hidden_in, positions, attn_gain, qkv_weight, qkv_bias, out_weight, *rest):
    size, groups = lax.axis_size("fsdp"), lax.axis_size("seq")
    _, tokens, width = hidden_in.shape
    units = rest[1].shape[0]
    if groups != 4 or size != 8 or tokens % 256 or units % 160 or width % 512:
        return False
    if (width // size) % 32 or qkv_bias.shape[0] > 256 or KV_HEADS != 2:
        return False
    rows = tokens * width * (4 * size + 34)
    return rows + units * (18 * width + 6 * tokens) < 64_000_000


def group_columns(array, seq):
    width_query = HEADS * HEAD_DIM
    own = width_query // 4
    kv_head = seq // 2
    parts = (
        (seq * own, own),
        (width_query + kv_head * HEAD_DIM, HEAD_DIM),
        (width_query + (KV_HEADS + kv_head) * HEAD_DIM, HEAD_DIM),
    )
    return jnp.concatenate(
        [lax.dynamic_slice_in_dim(array, at, count, array.ndim - 1) for at, count in parts], -1
    )


def per_device_kernels(
    hidden_in,
    positions,
    attn_gain,
    qkv_weight,
    qkv_bias,
    out_weight,
    mlp_gain,
    gate_weight,
    up_weight,
    down_weight,
    cotangent,
):
    f32, bf16 = jnp.float32, jnp.bfloat16
    groups = lax.axis_size("seq")
    size = lax.axis_size("fsdp")
    seq = lax.axis_index("seq")
    _, tokens, width = hidden_in.shape
    length = tokens * groups
    own = width // groups
    used = own + 2 * HEAD_DIM
    cosine, sine = rope_tables(positions[0])
    half_dim = HEAD_DIM // 2
    trig = jnp.concatenate([cosine[:, :half_dim], sine[:, half_dim:]], axis=1)
    piece = jnp.concatenate(
        [
            group_columns(qkv_weight, seq),
            lax.dynamic_slice_in_dim(out_weight, seq * own, own, 1),
        ],
        axis=1,
    )
    small_width = 256
    small = jnp.stack(
        [
            jnp.pad(row, (0, small_width - row.shape[0]))
            for row in (attn_gain, mlp_gain, qkv_bias)
        ]
    )
    small = jnp.pad(small, ((0, 13), (0, 0)))
    (
        normed_one,
        heads,
        attended,
        logs,
        weight,
        proj,
        trig_all,
        gains,
        normed_two,
        residual,
        all_cots,
    ) = attend_group(hidden_in[0], trig, piece, small, cotangent[0], qkv_bias.shape[0])
    shard = width // size
    outs, grad_residual, term_gain_two, unit_sums, far_gate = mlp_ring(
        normed_two,
        residual,
        gains[1:2],
        all_cots.reshape(size * tokens, width),
        gate_weight,
        up_weight,
        down_weight,
    )
    (
        grad_rows,
        hidden_out,
        smalls,
        shards,
        halves,
        far_sums,
        unit_sums,
        far_gate,
    ) = attend_group_backward(
        heads,
        attended,
        logs,
        proj,
        weight,
        normed_one,
        trig_all.reshape(length, HEAD_DIM),
        hidden_in[0],
        grad_residual,
        gains[0:1],
        term_gain_two,
        residual,
        outs,
        unit_sums,
        far_gate,
    )
    grad_gate, grad_up, grad_down, grad_rows, hidden_out, grad_qkv, grad_out = finish_totals(
        unit_sums, far_gate, far_sums, grad_rows, hidden_out, shards, halves
    )
    me = lax.axis_index("fsdp")
    bias_sums = jnp.concatenate([smalls[2], smalls[3, : 2 * KV_HEADS * HEAD_DIM]])
    bias_shard = qkv_bias.shape[0]
    return (
        hidden_out[None],
        grad_rows[None],
        lax.dynamic_slice_in_dim(smalls[0], me * shard, shard),
        grad_qkv,
        lax.dynamic_slice_in_dim(bias_sums, me * bias_shard, bias_shard),
        grad_out,
        lax.dynamic_slice_in_dim(smalls[1], me * shard, shard),
        grad_gate,
        grad_up,
        grad_down,
    )


def per_device_gathered(
    hidden_in,
    positions,
    attn_gain,
    qkv_weight,
    qkv_bias,
    out_weight,
    mlp_gain,
    gate_weight,
    up_weight,
    down_weight,
    cotangent,
):
    groups = lax.axis_size("seq")
    group_heads = HEADS // groups
    repeat = groups // KV_HEADS
    tokens = hidden_in.shape[1]
    width_query = HEADS * HEAD_DIM
    width_key = KV_HEADS * HEAD_DIM
    residual = hidden_in[0].astype(jnp.float32)
    cosine, sine = rope_tables(positions[0])
    gains_one, gains_two, qkv_full, bias_full, out_full = (
        lax.all_gather(attn_gain, "fsdp", axis=0, tiled=True),
        lax.all_gather(mlp_gain, "fsdp", axis=0, tiled=True),
        lax.all_gather(qkv_weight, "fsdp", axis=0, tiled=True),
        lax.all_gather(qkv_bias, "fsdp", axis=0, tiled=True),
        lax.all_gather(out_weight, "fsdp", axis=0, tiled=True),
    )
    gain_one = gains_one.astype(jnp.float32)
    gain_two = gains_two.astype(jnp.float32)
    unit_one, inverse_one, normed_one = norm_forward(residual, gain_one)
    qkv_mixed = jnp.dot(
        normed_one, qkv_full, preferred_element_type=jnp.float32
    ) + bias_full.astype(jnp.float32)
    query_part = qkv_mixed[:, :width_query].reshape(tokens, HEADS, HEAD_DIM)
    key_part = qkv_mixed[:, width_query : width_query + width_key].reshape(
        tokens, KV_HEADS, HEAD_DIM
    )
    value_part = qkv_mixed[:, width_query + width_key :].reshape(tokens, KV_HEADS, HEAD_DIM)
    queries = (
        rotate(query_part, cosine, sine)
        .astype(jnp.bfloat16)
        .reshape(tokens, groups, group_heads * HEAD_DIM)
    )
    keys_rep = jnp.repeat(rotate(key_part, cosine, sine).astype(jnp.bfloat16), repeat, axis=1)
    values_rep = jnp.repeat(value_part.astype(jnp.bfloat16), repeat, axis=1)
    head_queries, head_keys, head_values = (
        lax.all_to_all(queries, "seq", split_axis=1, concat_axis=0, tiled=True),
        lax.all_to_all(keys_rep, "seq", split_axis=1, concat_axis=0, tiled=True),
        lax.all_to_all(values_rep, "seq", split_axis=1, concat_axis=0, tiled=True),
    )
    head_queries = head_queries.reshape(-1, group_heads, HEAD_DIM)
    head_keys = head_keys.reshape(-1, HEAD_DIM)
    head_values = head_values.reshape(-1, HEAD_DIM)
    attended, log_totals = attend_forward(head_queries, head_keys, head_values)
    returned = lax.all_to_all(
        attended.reshape(-1, 1, group_heads * HEAD_DIM),
        "seq",
        split_axis=0,
        concat_axis=1,
        tiled=True,
    )
    attn_rows = returned.reshape(tokens, width_query)
    residual_two = residual + jnp.dot(attn_rows, out_full, preferred_element_type=jnp.float32)
    unit_two, inverse_two, normed_two = norm_forward(residual_two, gain_two)
    grad_output = cotangent[0].astype(jnp.float32)
    grad_mlp = grad_output.astype(jnp.bfloat16)
    all_rows = lax.all_gather(normed_two, "fsdp", axis=0, tiled=True)
    gate_pre = jnp.einsum("td,fd->tf", all_rows, gate_weight, preferred_element_type=jnp.float32)
    up_pre = jnp.einsum("td,fd->tf", all_rows, up_weight, preferred_element_type=jnp.float32)
    sigmoid_gate = jax.nn.sigmoid(gate_pre)
    activated = gate_pre * sigmoid_gate
    hidden = (activated * up_pre).astype(jnp.bfloat16)
    partial_out = jnp.dot(hidden, down_weight, preferred_element_type=jnp.float32)
    mlp_out = lax.psum_scatter(
        partial_out.astype(jnp.bfloat16), "fsdp", scatter_dimension=0, tiled=True
    ).astype(jnp.float32)
    all_grads = lax.all_gather(grad_mlp, "fsdp", axis=0, tiled=True)
    grad_hidden = jnp.einsum(
        "tm,fm->tf", all_grads, down_weight, preferred_element_type=jnp.float32
    )
    grad_gate = (
        grad_hidden * up_pre * sigmoid_gate * (1.0 + gate_pre * (1.0 - sigmoid_gate))
    ).astype(jnp.bfloat16)
    grad_up = (grad_hidden * activated).astype(jnp.bfloat16)
    partial_back = jnp.dot(grad_gate, gate_weight, preferred_element_type=jnp.float32) + jnp.dot(
        grad_up, up_weight, preferred_element_type=jnp.float32
    )
    grad_normed_two = lax.psum_scatter(partial_back, "fsdp", scatter_dimension=0, tiled=True)
    shard_gate = jnp.einsum("tf,td->fd", grad_gate, all_rows, preferred_element_type=jnp.float32)
    shard_up = jnp.einsum("tf,td->fd", grad_up, all_rows, preferred_element_type=jnp.float32)
    shard_down = jnp.einsum("tf,td->fd", hidden, all_grads, preferred_element_type=jnp.float32)
    hidden_out = (residual_two + mlp_out).astype(jnp.bfloat16)
    grad_norm_two, term_gain_two = norm_backward(grad_normed_two, unit_two, inverse_two, gain_two)
    grad_residual_two = grad_output + grad_norm_two
    grad_proj = grad_residual_two.astype(jnp.bfloat16)
    grad_attn_rows = jnp.einsum(
        "td,ed->te", grad_proj, out_full, preferred_element_type=jnp.float32
    ).astype(jnp.bfloat16)
    term_out = jnp.einsum("te,td->ed", attn_rows, grad_proj, preferred_element_type=jnp.float32)
    grad_heads = lax.all_to_all(
        grad_attn_rows.reshape(tokens, groups, group_heads * HEAD_DIM),
        "seq",
        split_axis=1,
        concat_axis=0,
        tiled=True,
    )
    grad_query, grad_keys, grad_values = attend_backward(
        head_queries,
        head_keys,
        head_values,
        log_totals,
        grad_heads.reshape(-1, group_heads, HEAD_DIM),
    )
    back_query, back_keys, back_values = (
        lax.all_to_all(
            grad_query.astype(jnp.bfloat16).reshape(-1, 1, group_heads * HEAD_DIM),
            "seq",
            split_axis=0,
            concat_axis=1,
            tiled=True,
        ),
        lax.all_to_all(
            grad_keys.astype(jnp.bfloat16)[:, None, :],
            "seq",
            split_axis=0,
            concat_axis=1,
            tiled=True,
        ),
        lax.all_to_all(
            grad_values.astype(jnp.bfloat16)[:, None, :],
            "seq",
            split_axis=0,
            concat_axis=1,
            tiled=True,
        ),
    )
    grad_query_rows = unrotate(
        back_query.reshape(tokens, HEADS, HEAD_DIM).astype(jnp.float32), cosine, sine
    )
    grad_key_rows = unrotate(
        jnp.sum(back_keys.astype(jnp.float32).reshape(tokens, KV_HEADS, repeat, HEAD_DIM), axis=2),
        cosine,
        sine,
    )
    grad_value_rows = jnp.sum(
        back_values.astype(jnp.float32).reshape(tokens, KV_HEADS, repeat, HEAD_DIM), axis=2
    )
    grad_mixed = jnp.concatenate(
        [
            grad_query_rows.reshape(tokens, width_query),
            grad_key_rows.reshape(tokens, width_key),
            grad_value_rows.reshape(tokens, width_key),
        ],
        axis=1,
    ).astype(jnp.bfloat16)
    term_qkv = jnp.einsum("td,tc->dc", normed_one, grad_mixed, preferred_element_type=jnp.float32)
    term_bias = jnp.sum(grad_mixed.astype(jnp.float32), axis=0)
    grad_normed_one = jnp.einsum(
        "tc,dc->td", grad_mixed, qkv_full, preferred_element_type=jnp.float32
    )
    grad_norm_one, term_gain_one = norm_backward(grad_normed_one, unit_one, inverse_one, gain_one)
    grad_rows = grad_residual_two + grad_norm_one
    shard_gain_one, shard_qkv, shard_bias, shard_out, shard_gain_two = (
        lax.psum_scatter(
            term_gain_one.astype(jnp.bfloat16), "fsdp", scatter_dimension=0, tiled=True
        ).astype(jnp.float32),
        lax.psum_scatter(
            term_qkv.astype(jnp.bfloat16), "fsdp", scatter_dimension=0, tiled=True
        ).astype(jnp.float32),
        lax.psum_scatter(
            term_bias.astype(jnp.bfloat16), "fsdp", scatter_dimension=0, tiled=True
        ).astype(jnp.float32),
        lax.psum_scatter(
            term_out.astype(jnp.bfloat16), "fsdp", scatter_dimension=0, tiled=True
        ).astype(jnp.float32),
        lax.psum_scatter(
            term_gain_two.astype(jnp.bfloat16), "fsdp", scatter_dimension=0, tiled=True
        ).astype(jnp.float32),
    )
    totals = (
        lax.psum(shard_gain_one.astype(jnp.bfloat16), "seq").astype(jnp.float32),
        lax.psum(shard_qkv.astype(jnp.bfloat16), "seq").astype(jnp.float32),
        lax.psum(shard_bias.astype(jnp.bfloat16), "seq").astype(jnp.float32),
        lax.psum(shard_out.astype(jnp.bfloat16), "seq").astype(jnp.float32),
        lax.psum(shard_gain_two.astype(jnp.bfloat16), "seq").astype(jnp.float32),
        lax.psum(shard_gate.astype(jnp.bfloat16), "seq").astype(jnp.float32),
        lax.psum(shard_up.astype(jnp.bfloat16), "seq").astype(jnp.float32),
        lax.psum(shard_down.astype(jnp.bfloat16), "seq").astype(jnp.float32),
    )
    return (
        hidden_out[None],
        grad_rows[None],
        totals[0],
        totals[1],
        totals[2],
        totals[3],
        totals[4],
        totals[5],
        totals[6],
        totals[7],
    )


def per_device(*arguments):
    return (per_device_kernels if kernels_fit(*arguments) else per_device_gathered)(*arguments)


def solution(mesh):
    placed = (
        P("fsdp", "seq", None),
        P("fsdp", "seq"),
        P("fsdp"),
        P("fsdp", None),
        P("fsdp"),
        P("fsdp", None),
        P("fsdp"),
        P("fsdp", None),
        P("fsdp", None),
        P("fsdp", None),
        P("fsdp", "seq", None),
    )
    return jax.shard_map(
        per_device,
        mesh=mesh,
        in_specs=placed,
        out_specs=(
            P("fsdp", "seq", None),
            P("fsdp", "seq", None),
            P("fsdp"),
            P("fsdp", None),
            P("fsdp"),
            P("fsdp", None),
            P("fsdp"),
            P("fsdp", None),
            P("fsdp", None),
            P("fsdp", None),
        ),
        check_vma=False,
    )
```

profile of v0, /device:TPU:2, one launch (start us, length us, event | category | flops | bytes accessed | tf_op | source)
XLA Modules:
  0.0 421.3 jit_solution(9100353959627312943)
XLA Ops:
  0.7 0.8 constant_dynamic-slice_fusion.4
  1.5 1.0 constant_dynamic-slice_fusion.2
  2.5 0.8 pad_maximum_fusion.piece_ref
  3.3 0.7 convert_element_type.15
  4.0 0.1 broadcast_multiply_fusion
  4.1 0.9 maximum_cosine_fusion
  5.0 0.8 pad_maximum_fusion.2.trig_ref
  5.8 0.7 pad.11
  6.5 0.7 pad.12
  7.1 0.7 stack.14
  7.8 0.6 fusion.5.small_ref
  8.4 104.8 %attend_forward.1 = (bf16[1024,1536]{1,0:T(8,128)(2,1)}, bf16[1024,640]{1,0:T(8,128)(2,1)}, bf16[1024,384]{1,0:T(8,128)(2,1)}, f32[1024,128]{1,0:T(8,128)}, bf16...) custom-call(bf16[256,1536]{1,0:T(8,128)(2,1)} %bitcast.11, ...), custom_call_target="tpu_custom_call" | custom-call | tf_op jit(solution)/shard_map/attend_forward/pallas_call | solution.py:593
  113.2 1.5 fusion.8
  114.7 145.0 %mlp_ring.1 = (bf16[2048,1536]{1,0:T(8,128)(2,1)}, f32[256,1536]{1,0:T(8,128)}, f32[1,1536]{1,0:T(1,128)}, bf16[3,1120,1536]{2,1,0:T(8,128)(2,1)}, bf16[1120,1536]{1,0:T(8,128)(2,1)}) custom-call(bf16[256,1536]{1,0:T(8,128)(2,1)} %get-tuple-element.48.normed_ref, f32[256,1536]{1,0:T(8,128)} %get-tuple-element.49.resid_ref, ...), custom_call_target="tpu_custom_call" | custom-call | tf_op jit(solution)/shard_map/mlp_ring/pallas_call | solution.py:943
  259.7 139.0 %attend_backward.1 = (f32[256,1536]{1,0:T(8,128)}, bf16[256,1536]{1,0:T(8,128)(2,1)}, f32[8,1536]{1,0:T(8,128)}, bf16[4,192,640]{2,1,0:T(8,128)(2,1)}, bf16[2,19...) custom-call(bf16[1024,640]{1,0:T(8,128)(2,1)} %get-tuple-element.41., ...), custom_call_target="tpu_custom_call", output_to_operand_aliasing={{6}: (13, {}), {7}: (14, {})} | custom-call | tf_op jit(solution)/shard_map/attend_backward/pallas_call | solution.py:1548
  398.7 0.9 fusion.7
  399.7 0.7 slice.30
  400.4 0.6 fusion.6
  401.0 19.0 %finish_totals.1 = (f32[1120,1536]{1,0:T(8,128)}, f32[1120,1536]{1,0:T(8,128)}, f32[1120,1536]{1,0:T(8,128)}, f32[256,1536]{1,0:T(8,128)}, bf16[256,1536]{1,0:T(...) custom-call(bf16[3,1120,1536]{2,1,0:T(8,128)(2,1)} %get-tuple-element.57.sums_ref, ...), custom_call_target="tpu_custom_call" | custom-call | tf_op jit(solution)/shard_map/finish_totals/pallas_call | solution.py:1679
  420.0 0.6 constant_dynamic-slice_fusion.1
  420.6 0.6 constant_dynamic-slice_fusion
  (3 shorter events, 0.0 us)
where the time goes:
time: 422 us; the launch traced here: 421 us
  Pallas kernels  408 us (97%)
  local copies, waits for them, and re-layouts  8.25 us (2%)
  other arithmetic  4.53 us (1%)
    pallas_call x1, Pallas kernels, mlp_ring(): pl.pallas_call(functools.partial(mlp_kernel, size), out_shape=(jax.ShapeD...  145 us
    pallas_call x1, Pallas kernels, attend_group_backward(): pl.pallas_call(functools.partial(attend_backward_kernel, size), out_shape...  139 us
    pallas_call x1, Pallas kernels, attend_group(): pl.pallas_call(functools.partial(attend_forward_kernel, size, tokens, bia...  105 us
    pallas_call x1, Pallas kernels, finish_totals(): pl.pallas_call(finish_kernel, grid=(steps,), out_shape=(jax.ShapeDtypeStr...  19 us

commit v1 on v0

--- a/solution.py
+++ b/solution.py
@@ -201,7 +201,8 @@
     bias_share,
     rows_ref,
     trig_ref,
-    piece_ref,
+    qkv_ref,
+    proj_ref,
     small_ref,
     cot_ref,
     normed_out,
@@ -233,6 +234,7 @@
     far_sum,
     normed_two,
     load_sems,
+    column_sems,
     store_sems,
     ring_sems,
     small_sems,
@@ -244,12 +246,12 @@
     proj_recv,
 ):
     f32, bf16 = jnp.float32, jnp.bfloat16
-    depth, joint = piece_ref.shape
+    depth = qkv_ref.shape[0]
     tokens, width = rows_ref.shape
     half = depth // 2
     cot_half = tokens // 2
     own = proj.shape[0]
-    used = joint - own
+    used = own + 2 * HEAD_DIM
     count = own // HEAD_DIM
     length = part.shape[0]
     per_group = own // depth
@@ -272,15 +274,36 @@
             device_id_type=MESH,
         )
 
+    width_query = 4 * own
+    own_lane = pl.multiple_of(seq * own, HEAD_DIM)
+    kv_lane = pl.multiple_of(width_query + (seq // 2) * HEAD_DIM, HEAD_DIM)
+    value_lane = pl.multiple_of(kv_lane + KV_HEADS * HEAD_DIM, HEAD_DIM)
+    my_rows = pl.ds(pl.multiple_of(me * depth, 16), depth)
+    column_loads = [
+        pltpu.make_async_copy(
+            source.at[:, pl.ds(lane_at, lanes)],
+            pieces.at[my_rows, pl.ds(target, lanes)],
+            column_sems.at[at],
+        )
+        for at, (source, lane_at, target, lanes) in enumerate(
+            (
+                (qkv_ref, own_lane, 0, own),
+                (qkv_ref, kv_lane, own, HEAD_DIM),
+                (qkv_ref, value_lane, own + HEAD_DIM, HEAD_DIM),
+                (proj_ref, own_lane, used, own),
+            )
+        )
+    ]
     loads = [
-        pltpu.make_async_copy(piece_ref, pieces.at[pl.ds(pl.multiple_of(me * depth, 16), depth)], load_sems.at[0]),
-        pltpu.make_async_copy(trig_ref, trig_all.at[seq], load_sems.at[1]),
-        pltpu.make_async_copy(rows_ref, rows_all.at[seq], load_sems.at[2]),
-        pltpu.make_async_copy(small_ref, smalls.at[me], load_sems.at[3]),
-        pltpu.make_async_copy(cot_ref, cots.at[me], load_sems.at[4]),
+        pltpu.make_async_copy(trig_ref, trig_all.at[seq], load_sems.at[0]),
+        pltpu.make_async_copy(rows_ref, rows_all.at[seq], load_sems.at[1]),
+        pltpu.make_async_copy(cot_ref, cots.at[me], load_sems.at[2]),
     ]
-    for load in loads:
+    for load in column_loads + loads:
         load.start()
+    smalls[me] = jnp.zeros(smalls.shape[1:], f32)
+    for at in range(3):
+        smalls[me, at : at + 1, :] = small_ref[:, at * 256 : (at + 1) * 256]
     greet(ring + ({"seq": core}, {"seq": far}, {"seq": diagonal}))
 
     def piece_of(step, side):
@@ -367,19 +390,19 @@
         for side in range(2):
             cot_store(step, side).start()
 
-    loads[0].wait()
+    for load in column_loads:
+        load.wait()
     for sub in range(2):
         for side in range(2):
             ring_copy(0, side, sub).start()
-    loads[3].wait()
     small_copy(0).start()
     for which in (1, 0):
-        loads[2 - which].wait()
+        loads[1 - which].wait()
         seq_copy(which, seq, far, 1).start()
         seq_copy(which, seq, core, 0).start()
     for side in range(2):
         proj_act(0, side, "start")
-    loads[4].wait()
+    loads[2].wait()
 
     for step in range(size - 1):
         for sub in range(2):
@@ -402,7 +425,7 @@
     gathered = jnp.zeros((8, width), f32)
     small_width = smalls.shape[2]
     for at in range(size):
-        held = smalls[at].astype(f32)[0:8, :]
+        held = smalls[at]
         lane = lax.broadcasted_iota(jnp.int32, held.shape, 1)
         wide = jnp.concatenate(
             [
@@ -423,12 +446,9 @@
     store(pieces, piece_out)
     store(trig_all, trig_out)
 
-    width_query = count * HEAD_DIM * 4
-    kv_lane = pl.multiple_of(width_query + (seq // 2) * HEAD_DIM, HEAD_DIM)
-    value_lane = pl.multiple_of(kv_lane + KV_HEADS * HEAD_DIM, HEAD_DIM)
     own_bias = jnp.concatenate(
         [
-            bias[2:3, pl.ds(pl.multiple_of(seq * own, HEAD_DIM), own)],
+            bias[2:3, pl.ds(own_lane, own)],
             bias[2:3, pl.ds(kv_lane, HEAD_DIM)],
             bias[2:3, pl.ds(value_lane, HEAD_DIM)],
         ],
@@ -545,13 +565,14 @@
         copy.wait()
 
 
-def attend_group(rows, trig, piece, small, cots, bias_share):
+def attend_group(rows, trig, qkv_weight, out_weight, small, bias_share, cots):
     size = lax.axis_size("fsdp")
     groups = lax.axis_size("seq")
     tokens, width = rows.shape
-    depth, joint = piece.shape
+    depth = qkv_weight.shape[0]
     own = width // groups
-    used = joint - own
+    used = own + 2 * HEAD_DIM
+    joint = used + own
     length = tokens * groups
     f32, bf16 = jnp.float32, jnp.bfloat16
     dma = pltpu.SemaphoreType.DMA
@@ -576,7 +597,7 @@
         trig_all,
         pieces,
         proj,
-        ((size,) + small.shape, bf16),
+        ((size, 8, 256), f32),
         cots_all,
         normed,
         heads,
@@ -593,11 +614,12 @@
     return pl.pallas_call(
         functools.partial(attend_forward_kernel, size, tokens, bias_share),
         out_shape=tuple(jax.ShapeDtypeStruct(*shape) for shape in outs),
-        in_specs=[anywhere] * 5,
+        in_specs=[anywhere] * 4 + [pl.BlockSpec(memory_space=pltpu.VMEM), anywhere],
         out_specs=(anywhere,) * len(outs),
         scratch_shapes=[pltpu.VMEM(*shape) for shape in held]
         + [
-            dma((5,)),
+            dma((3,)),
+            dma((4,)),
             dma((len(outs),)),
             dma((2, 2, 2, size)),
             dma((2, size)),
@@ -612,7 +634,14 @@
             collective_id=1, has_side_effects=True, vmem_limit_bytes=VMEM_BYTES
         ),
         name="attend_forward",
-    )(rows, trig, piece, small, cots)
+    )(
+        rows,
+        trig,
+        qkv_weight,
+        out_weight,
+        small,
+        cots,
+    )
 
 
 CHUNKS = 5
@@ -909,7 +938,7 @@
     inverse = inverse_of(resid[...])
     unit_rows = resid[...] * inverse
     gain_grad_ref[...] = jnp.sum(grad_normed * unit_rows, axis=0, keepdims=True)
-    grad_unit = grad_normed * gain_ref[...]
+    grad_unit = grad_normed * gain_ref[1:2, :]
     cot_own.wait()
     back_ref[...] = cots[0].astype(jnp.float32) + inverse * (
         grad_unit - unit_rows * jnp.mean(grad_unit * unit_rows, axis=-1, keepdims=True)
@@ -1380,6 +1409,7 @@
     half_step(2)
     out_step(5)
     to_core[1].wait_recv()
+    send_units(1)
     to_far.wait_recv()
     rows = hidden_ref[...].astype(f32)
     inverse = lax.rsqrt(jnp.mean(rows * rows, axis=-1, keepdims=True) + norm_eps)
@@ -1389,7 +1419,7 @@
     )
     small_in[0, 0:1, :] = jnp.sum(grad_rows * unit_rows, axis=0, keepdims=True)
     small_copy(0).start()
-    grad_unit = grad_rows * gain_ref[...]
+    grad_unit = grad_rows * gain_ref[0:1, :]
     grad_in_ref[...] = resid_grad_ref[...] + inverse * (
         grad_unit - unit_rows * jnp.mean(grad_unit * unit_rows, axis=-1, keepdims=True)
     )
@@ -1397,7 +1427,7 @@
     small_step(0)
     small_copy(1).start()
     done = 1
-    send_units(3)
+    send_units(2)
     for step in range(3, size):
         term_step(step)
         half_step(step)
@@ -1666,7 +1696,7 @@
     groups, depth, used = shards.shape
     joint = groups * (used - 2 * HEAD_DIM) + 2 * KV_HEADS * HEAD_DIM
     tokens = grad_in.shape[0]
-    steps, few = 10, 8
+    steps, few = 5, 4
 
     def spec(*dims, many=False):
         lead = len(dims) - 2
@@ -1723,20 +1753,6 @@
     return rows + units * (18 * width + 6 * tokens) < 64_000_000
 
 
-def group_columns(array, seq):
-    width_query = HEADS * HEAD_DIM
-    own = width_query // 4
-    kv_head = seq // 2
-    parts = (
-        (seq * own, own),
-        (width_query + kv_head * HEAD_DIM, HEAD_DIM),
-        (width_query + (KV_HEADS + kv_head) * HEAD_DIM, HEAD_DIM),
-    )
-    return jnp.concatenate(
-        [lax.dynamic_slice_in_dim(array, at, count, array.ndim - 1) for at, count in parts], -1
-    )
-
-
 def per_device_kernels(
     hidden_in,
     positions,
@@ -1753,29 +1769,20 @@
     f32, bf16 = jnp.float32, jnp.bfloat16
     groups = lax.axis_size("seq")
     size = lax.axis_size("fsdp")
-    seq = lax.axis_index("seq")
     _, tokens, width = hidden_in.shape
     length = tokens * groups
-    own = width // groups
-    used = own + 2 * HEAD_DIM
-    cosine, sine = rope_tables(positions[0])
-    half_dim = HEAD_DIM // 2
-    trig = jnp.concatenate([cosine[:, :half_dim], sine[:, half_dim:]], axis=1)
-    piece = jnp.concatenate(
+    lane = jnp.arange(HEAD_DIM)
+    frequency = jnp.exp(
+        -((lane % (HEAD_DIM // 2)).astype(f32) * 2.0 / HEAD_DIM) * math.log(rope_base)
+    )
+    angles = positions[0].astype(f32)[:, None] * frequency[None, :]
+    trig = jnp.where(lane[None, :] < HEAD_DIM // 2, jnp.cos(angles), jnp.sin(angles))
+    small = jnp.concatenate(
         [
-            group_columns(qkv_weight, seq),
-            lax.dynamic_slice_in_dim(out_weight, seq * own, own, 1),
-        ],
-        axis=1,
-    )
-    small_width = 256
-    small = jnp.stack(
-        [
-            jnp.pad(row, (0, small_width - row.shape[0]))
+            jnp.pad(row.astype(f32), (0, 256 - row.shape[0]))
             for row in (attn_gain, mlp_gain, qkv_bias)
         ]
-    )
-    small = jnp.pad(small, ((0, 13), (0, 0)))
+    )[None]
     (
         normed_one,
         heads,
@@ -1788,12 +1795,14 @@
         normed_two,
         residual,
         all_cots,
-    ) = attend_group(hidden_in[0], trig, piece, small, cotangent[0], qkv_bias.shape[0])
+    ) = attend_group(
+        hidden_in[0], trig, qkv_weight, out_weight, small, qkv_bias.shape[0], cotangent[0]
+    )
     shard = width // size
     outs, grad_residual, term_gain_two, unit_sums, far_gate = mlp_ring(
         normed_two,
         residual,
-        gains[1:2],
+        gains,
         all_cots.reshape(size * tokens, width),
         gate_weight,
         up_weight,
@@ -1818,7 +1827,7 @@
         trig_all.reshape(length, HEAD_DIM),
         hidden_in[0],
         grad_residual,
-        gains[0:1],
+        gains,
         term_gain_two,
         residual,
         outs,

time: 422 us -> 410 us (0.972)
  local copies, waits for them, and re-layouts: 8.25 us -> 2.88 us
  Pallas kernels: 408 us -> 403 us
    pallas_call x1, Pallas kernels: 139 us -> 134 us  [attend_group_backward(): pl.pallas_call(functools.partial(attend_backward_kernel, size), out_shape...]
where the time goes in v1:
time: 410 us
  Pallas kernels  403 us (98%)
    pallas_call x1, Pallas kernels, mlp_ring(): pl.pallas_call(functools.partial(mlp_kernel, size), out_shape=(jax.ShapeD...  145 us
    pallas_call x1, Pallas kernels, attend_group_backward(): pl.pallas_call(functools.partial(attend_backward_kernel, size), out_shape...  134 us
    pallas_call x1, Pallas kernels, attend_group(): pl.pallas_call(functools.partial(attend_forward_kernel, size, tokens, bia...  105 us
    pallas_call x1, Pallas kernels, finish_totals(): pl.pallas_call(finish_kernel, grid=(steps,), out_shape=(jax.ShapeDtypeStr...  17.8 us

profile of v1, /device:TPU:2, one launch (start us, length us, event | category | flops | bytes accessed | tf_op | source)
XLA Modules:
  0.0 409.7 jit_solution(9827981187254588599)
XLA Ops:
  0.6 0.7 convert_element_type.23
  1.3 1.2 fusion.trig_ref
  2.5 0.7 fusion.6
  3.2 0.6 reshape.55.small_ref
  3.8 105.5 %attend_forward.1 = (bf16[1024,1536]{1,0:T(8,128)(2,1)}, bf16[1024,640]{1,0:T(8,128)(2,1)}, bf16[1024,384]{1,0:T(8,128)(2,1)}, f32[1024,128]{1,0:T(8,128)}, bf16...) custom-call(bf16[256,1536]{1,0:T(8,128)(2,1)} %bitcast.11, ...), custom_call_target="tpu_custom_call" | custom-call | tf_op jit(solution)/shard_map/attend_forward/pallas_call | solution.py:614
  109.3 145.2 %mlp_ring.1 = (bf16[2048,1536]{1,0:T(8,128)(2,1)}, f32[256,1536]{1,0:T(8,128)}, f32[1,1536]{1,0:T(1,128)}, bf16[3,1120,1536]{2,1,0:T(8,128)(2,1)}, bf16[1120,1536]{1,0:T(8,128)(2,1)}) custom-call(bf16[256,1536]{1,0:T(8,128)(2,1)} %get-tuple-element.48.normed_ref, f32[256,1536]{1,0:T(8,128)} %get-tuple-element.49.resid_ref, ...), custom_call_target="tpu_custom_call" | custom-call | tf_op jit(solution)/shard_map/mlp_ring/pallas_call | solution.py:972
  254.5 134.3 %attend_backward.1 = (f32[256,1536]{1,0:T(8,128)}, bf16[256,1536]{1,0:T(8,128)(2,1)}, f32[8,1536]{1,0:T(8,128)}, bf16[4,192,640]{2,1,0:T(8,128)(2,1)}, bf16[2,19...) custom-call(bf16[1024,640]{1,0:T(8,128)(2,1)} %get-tuple-element.41., ...), custom_call_target="tpu_custom_call", output_to_operand_aliasing={{6}: (13, {}), {7}: (14, {})} | custom-call | tf_op jit(solution)/shard_map/attend_backward/pallas_call | solution.py:1578
  388.8 0.9 fusion.13
  389.8 0.7 slice.14
  390.5 0.6 fusion.7
  391.1 0.6 constant_dynamic-slice_fusion
  391.8 17.8 %finish_totals.1 = (f32[1120,1536]{1,0:T(8,128)}, f32[1120,1536]{1,0:T(8,128)}, f32[1120,1536]{1,0:T(8,128)}, f32[256,1536]{1,0:T(8,128)}, bf16[256,1536]{1,0:T(...) custom-call(bf16[3,1120,1536]{2,1,0:T(8,128)(2,1)} %get-tuple-element.57.sums_ref, ...), custom_call_target="tpu_custom_call" | custom-call | tf_op jit(solution)/shard_map/finish_totals/pallas_call | solution.py:1709
  (2 shorter events, 0.0 us)

commit v2 on v1

--- a/solution.py
+++ b/solution.py
@@ -413,7 +413,7 @@
         small_copy(step).wait_recv()
         if step < size - 2:
             small_copy(step + 1).start()
-        if step == size - 3:
+        if step == 1:
             cot_pump(0)
         for side in range(2):
             proj_act(step + 1, side, "start")
@@ -466,7 +466,7 @@
                 turned * cosine + pltpu.roll(turned, HEAD_DIM // 2, 1) * sine
             ).astype(bf16)
         heads[span, head_columns(count + 1)] = mixed[:, head_columns(count + 1)].astype(bf16)
-        if 2 * (at + 1) == length // block:
+        if at == 0:
             cot_pump(1)
     store(normed, normed_out)
     store(heads, heads_out)

time: 410 us -> 404 us (0.985)
  Pallas kernels: 403 us -> 397 us
    pallas_call x1, Pallas kernels: 105 us -> 99.1 us  [attend_group(): pl.pallas_call(functools.partial(attend_forward_kernel, size, tokens, bia...]
where the time goes in v2:
time: 404 us
  Pallas kernels  397 us (98%)
    pallas_call x1, Pallas kernels, mlp_ring(): pl.pallas_call(functools.partial(mlp_kernel, size), out_shape=(jax.ShapeD...  146 us
    pallas_call x1, Pallas kernels, attend_group_backward(): pl.pallas_call(functools.partial(attend_backward_kernel, size), out_shape...  134 us
    pallas_call x1, Pallas kernels, attend_group(): pl.pallas_call(functools.partial(attend_forward_kernel, size, tokens, bia...  99.1 us
    pallas_call x1, Pallas kernels, finish_totals(): pl.pallas_call(finish_kernel, grid=(steps,), out_shape=(jax.ShapeDtypeStr...  17.8 us

profile of v2, /device:TPU:2, one launch (start us, length us, event | category | flops | bytes accessed | tf_op | source)
XLA Modules:
  0.0 403.6 jit_solution(953703535990801285)
XLA Ops:
  0.6 0.7 convert_element_type.23
  1.3 1.2 fusion.trig_ref
  2.5 0.7 fusion.6
  3.2 0.6 reshape.55.small_ref
  3.8 99.1 %attend_forward.1 = (bf16[1024,1536]{1,0:T(8,128)(2,1)}, bf16[1024,640]{1,0:T(8,128)(2,1)}, bf16[1024,384]{1,0:T(8,128)(2,1)}, f32[1024,128]{1,0:T(8,128)}, bf16...) custom-call(bf16[256,1536]{1,0:T(8,128)(2,1)} %bitcast.11, ...), custom_call_target="tpu_custom_call" | custom-call | tf_op jit(solution)/shard_map/attend_forward/pallas_call | solution.py:614
  103.0 145.9 %mlp_ring.1 = (bf16[2048,1536]{1,0:T(8,128)(2,1)}, f32[256,1536]{1,0:T(8,128)}, f32[1,1536]{1,0:T(1,128)}, bf16[3,1120,1536]{2,1,0:T(8,128)(2,1)}, bf16[1120,1536]{1,0:T(8,128)(2,1)}) custom-call(bf16[256,1536]{1,0:T(8,128)(2,1)} %get-tuple-element.48.normed_ref, f32[256,1536]{1,0:T(8,128)} %get-tuple-element.49.resid_ref, ...), custom_call_target="tpu_custom_call" | custom-call | tf_op jit(solution)/shard_map/mlp_ring/pallas_call | solution.py:972
  248.9 133.8 %attend_backward.1 = (f32[256,1536]{1,0:T(8,128)}, bf16[256,1536]{1,0:T(8,128)(2,1)}, f32[8,1536]{1,0:T(8,128)}, bf16[4,192,640]{2,1,0:T(8,128)(2,1)}, bf16[2,19...) custom-call(bf16[1024,640]{1,0:T(8,128)(2,1)} %get-tuple-element.41., ...), custom_call_target="tpu_custom_call", output_to_operand_aliasing={{6}: (13, {}), {7}: (14, {})} | custom-call | tf_op jit(solution)/shard_map/attend_backward/pallas_call | solution.py:1578
  382.7 0.9 fusion.13
  383.6 0.7 slice.14
  384.4 0.6 fusion.7
  385.0 0.6 constant_dynamic-slice_fusion
  385.6 17.8 %finish_totals.1 = (f32[1120,1536]{1,0:T(8,128)}, f32[1120,1536]{1,0:T(8,128)}, f32[1120,1536]{1,0:T(8,128)}, f32[256,1536]{1,0:T(8,128)}, bf16[256,1536]{1,0:T(...) custom-call(bf16[3,1120,1536]{2,1,0:T(8,128)(2,1)} %get-tuple-element.57.sums_ref, ...), custom_call_target="tpu_custom_call" | custom-call | tf_op jit(solution)/shard_map/finish_totals/pallas_call | solution.py:1709
  (2 shorter events, 0.0 us)

commit v3 on v2

--- a/solution.py
+++ b/solution.py
@@ -1696,7 +1696,7 @@
     groups, depth, used = shards.shape
     joint = groups * (used - 2 * HEAD_DIM) + 2 * KV_HEADS * HEAD_DIM
     tokens = grad_in.shape[0]
-    steps, few = 5, 4
+    steps, few = 4, 4
 
     def spec(*dims, many=False):
         lead = len(dims) - 2

time: 404 us -> 402 us (level)
  no operation moved by 1% of the time
where the time goes in v3:
time: 402 us
  Pallas kernels  395 us (98%)
    pallas_call x1, Pallas kernels, mlp_ring(): pl.pallas_call(functools.partial(mlp_kernel, size), out_shape=(jax.ShapeD...  146 us
    pallas_call x1, Pallas kernels, attend_group_backward(): pl.pallas_call(functools.partial(attend_backward_kernel, size), out_shape...  134 us
    pallas_call x1, Pallas kernels, attend_group(): pl.pallas_call(functools.partial(attend_forward_kernel, size, tokens, bia...  99.1 us
    pallas_call x1, Pallas kernels, finish_totals(): pl.pallas_call(finish_kernel, grid=(steps,), out_shape=(jax.ShapeDtypeStr...  15.9 us

profile of v3, /device:TPU:2, one launch (start us, length us, event | category | flops | bytes accessed | tf_op | source)
XLA Modules:
  0.0 401.7 jit_solution(2684691124286489608)
XLA Ops:
  0.6 0.7 convert_element_type.23
  1.3 1.2 fusion.trig_ref
  2.5 0.7 fusion.6
  3.2 0.6 reshape.55.small_ref
  3.8 99.1 %attend_forward.1 = (bf16[1024,1536]{1,0:T(8,128)(2,1)}, bf16[1024,640]{1,0:T(8,128)(2,1)}, bf16[1024,384]{1,0:T(8,128)(2,1)}, f32[1024,128]{1,0:T(8,128)}, bf16...) custom-call(bf16[256,1536]{1,0:T(8,128)(2,1)} %bitcast.11, ...), custom_call_target="tpu_custom_call" | custom-call | tf_op jit(solution)/shard_map/attend_forward/pallas_call | solution.py:614
  103.0 145.9 %mlp_ring.1 = (bf16[2048,1536]{1,0:T(8,128)(2,1)}, f32[256,1536]{1,0:T(8,128)}, f32[1,1536]{1,0:T(1,128)}, bf16[3,1120,1536]{2,1,0:T(8,128)(2,1)}, bf16[1120,1536]{1,0:T(8,128)(2,1)}) custom-call(bf16[256,1536]{1,0:T(8,128)(2,1)} %get-tuple-element.48.normed_ref, f32[256,1536]{1,0:T(8,128)} %get-tuple-element.49.resid_ref, ...), custom_call_target="tpu_custom_call" | custom-call | tf_op jit(solution)/shard_map/mlp_ring/pallas_call | solution.py:972
  248.9 133.8 %attend_backward.1 = (f32[256,1536]{1,0:T(8,128)}, bf16[256,1536]{1,0:T(8,128)(2,1)}, f32[8,1536]{1,0:T(8,128)}, bf16[4,192,640]{2,1,0:T(8,128)(2,1)}, bf16[2,19...) custom-call(bf16[1024,640]{1,0:T(8,128)(2,1)} %get-tuple-element.41., ...), custom_call_target="tpu_custom_call", output_to_operand_aliasing={{6}: (13, {}), {7}: (14, {})} | custom-call | tf_op jit(solution)/shard_map/attend_backward/pallas_call | solution.py:1578
  382.7 0.9 fusion.13
  383.6 0.7 slice.14
  384.4 0.6 fusion.7
  385.0 0.6 constant_dynamic-slice_fusion
  385.6 15.9 %finish_totals.1 = (f32[1120,1536]{1,0:T(8,128)}, f32[1120,1536]{1,0:T(8,128)}, f32[1120,1536]{1,0:T(8,128)}, f32[256,1536]{1,0:T(8,128)}, bf16[256,1536]{1,0:T(...) custom-call(bf16[3,1120,1536]{2,1,0:T(8,128)(2,1)} %get-tuple-element.57.sums_ref, ...), custom_call_target="tpu_custom_call" | custom-call | tf_op jit(solution)/shard_map/finish_totals/pallas_call | solution.py:1709
  (2 shorter events, 0.0 us)

commit v4 on v3

--- a/solution.py
+++ b/solution.py
@@ -1436,7 +1436,7 @@
             done += 1
             if done < total_rounds:
                 small_copy(done).start()
-        if step == 4:
+        if step == 3:
             send_units(2)
         if step % 2 == 0:
             pass_units(2)

time: 402 us -> 402 us (level)
  no operation moved by 1% of the time
where the time goes in v4:
time: 402 us
  Pallas kernels  395 us (98%)
    pallas_call x1, Pallas kernels, mlp_ring(): pl.pallas_call(functools.partial(mlp_kernel, size), out_shape=(jax.ShapeD...  146 us
    pallas_call x1, Pallas kernels, attend_group_backward(): pl.pallas_call(functools.partial(attend_backward_kernel, size), out_shape...  134 us
    pallas_call x1, Pallas kernels, attend_group(): pl.pallas_call(functools.partial(attend_forward_kernel, size, tokens, bia...  99.1 us
    pallas_call x1, Pallas kernels, finish_totals(): pl.pallas_call(finish_kernel, grid=(steps,), out_shape=(jax.ShapeDtypeStr...  15.9 us

profile of v4, /device:TPU:2, one launch (start us, length us, event | category | flops | bytes accessed | tf_op | source)
XLA Modules:
  0.0 401.7 jit_solution(7996595161613605358)
XLA Ops:
  0.6 0.7 convert_element_type.23
  1.3 1.2 fusion.trig_ref
  2.5 0.7 fusion.6
  3.2 0.6 reshape.55.small_ref
  3.8 99.1 %attend_forward.1 = (bf16[1024,1536]{1,0:T(8,128)(2,1)}, bf16[1024,640]{1,0:T(8,128)(2,1)}, bf16[1024,384]{1,0:T(8,128)(2,1)}, f32[1024,128]{1,0:T(8,128)}, bf16...) custom-call(bf16[256,1536]{1,0:T(8,128)(2,1)} %bitcast.11, ...), custom_call_target="tpu_custom_call" | custom-call | tf_op jit(solution)/shard_map/attend_forward/pallas_call | solution.py:614
  103.0 145.9 %mlp_ring.1 = (bf16[2048,1536]{1,0:T(8,128)(2,1)}, f32[256,1536]{1,0:T(8,128)}, f32[1,1536]{1,0:T(1,128)}, bf16[3,1120,1536]{2,1,0:T(8,128)(2,1)}, bf16[1120,1536]{1,0:T(8,128)(2,1)}) custom-call(bf16[256,1536]{1,0:T(8,128)(2,1)} %get-tuple-element.48.normed_ref, f32[256,1536]{1,0:T(8,128)} %get-tuple-element.49.resid_ref, ...), custom_call_target="tpu_custom_call" | custom-call | tf_op jit(solution)/shard_map/mlp_ring/pallas_call | solution.py:972
  248.9 133.8 %attend_backward.1 = (f32[256,1536]{1,0:T(8,128)}, bf16[256,1536]{1,0:T(8,128)(2,1)}, f32[8,1536]{1,0:T(8,128)}, bf16[4,192,640]{2,1,0:T(8,128)(2,1)}, bf16[2,19...) custom-call(bf16[1024,640]{1,0:T(8,128)(2,1)} %get-tuple-element.41., ...), custom_call_target="tpu_custom_call", output_to_operand_aliasing={{6}: (13, {}), {7}: (14, {})} | custom-call | tf_op jit(solution)/shard_map/attend_backward/pallas_call | solution.py:1578
  382.7 0.9 fusion.13
  383.6 0.7 slice.14
  384.4 0.6 fusion.7
  385.0 0.6 constant_dynamic-slice_fusion
  385.6 15.9 %finish_totals.1 = (f32[1120,1536]{1,0:T(8,128)}, f32[1120,1536]{1,0:T(8,128)}, f32[1120,1536]{1,0:T(8,128)}, f32[256,1536]{1,0:T(8,128)}, bf16[256,1536]{1,0:T(...) custom-call(bf16[3,1120,1536]{2,1,0:T(8,128)(2,1)} %get-tuple-element.57.sums_ref, ...), custom_call_target="tpu_custom_call" | custom-call | tf_op jit(solution)/shard_map/finish_totals/pallas_call | solution.py:1709
  (2 shorter events, 0.0 us)
